TPU v7x, 256 devices: a whole 4x4x8 slice. The times are simulated.
256 devices in a mesh: rows: 32 (over z, x), cols: 8 (over y, core).
Axes of the slice: x: 4, y: 4, z: 8, core: 2. Of those that a mesh axis runs over, the one named last changes fastest.
Arguments:
- panel_t: float32 [16, 16384], P(None, ('rows', 'cols')), may hold values from -6 to 6
- kinship: float32 [16384, 16384], P('rows', 'cols'), may hold values from -0.046875 to 0.046875
Outputs:
- kin_panel_t: float32 [16, 16384], P(None, ('rows', 'cols'))
- score: float32 [16, 16], replicated
All inputs are finite; a program needn't handle non-finite values.
Results may differ from a plain program's by a relative error of at most 0.00008.
Values sent between devices are 32-bit elements; how exact they have to be, the bound alone decides.
No kernel may reach another device: no remote copies, remote signals or barrier semaphores. Data moves between devices by JAX's collectives and lax.ppermute only.
A program may use at most 64 MiB of HBM per device.

v0:
```python
import jax
import jax.numpy as jnp
from jax import lax
from jax.sharding import Mesh
from jax.sharding import PartitionSpec as P

COLS = ("cols_0", "cols_1")
ROWS_COLS = ("rows_0", "rows_1", "cols_0", "cols_1")
ROWS = ("rows_0", "rows_1")


def sent_to_all(x, axis):
    copies = jnp.broadcast_to(x, (lax.axis_size(axis), *x.shape))
    return lax.all_to_all(copies, axis, split_axis=0, concat_axis=0, tiled=True)


def in_order(tiles, dim):
    tiles = jnp.moveaxis(tiles, 0, dim)
    dims = tiles.shape
    return tiles.reshape(*dims[:dim], dims[dim] * dims[dim + 1], *dims[dim + 2 :])


def whole_of(x, axes, dim):
    far, near = axes
    leading = sent_to_all(x, far)
    tiles = jnp.swapaxes(sent_to_all(leading, near), 0, 1)
    return in_order(tiles.reshape(-1, *x.shape), dim)


def cut_along(x, dim, length):
    dims = x.shape
    tiles = x.reshape(*dims[:dim], length, dims[dim] // length, *dims[dim + 1 :])
    return jnp.moveaxis(tiles, dim, 0)


def sent_and_summed(x, axis, dim):
    length = lax.axis_size(axis)
    tiles = lax.all_to_all(cut_along(x, dim, length), axis, 0, 0, tiled=True)
    return jnp.sum(tiles, axis=0)


def taken_together(x, axis):
    return sent_to_all(x, axis).sum(axis=0)


def over_axes(x, axes):
    far, near = axes
    return taken_together(taken_together(x, near), far)


def contract(left, right):
    return lax.dot_general(
        left,
        right,
        (((1,), (1,)), ((), ())),
        precision=lax.Precision.HIGHEST,
        preferred_element_type=jnp.float32,
    )


def shards(panel_t, kinship):
    slab_rows, block_cols = kinship.shape
    col_index = lax.axis_index(COLS)
    gathered = whole_of(panel_t, (("rows_0", "rows_1"), ("cols_0", "cols_1")), 1)
    block_panel = lax.dynamic_slice_in_dim(gathered, col_index * block_cols, block_cols, 1)
    partial_value = contract(block_panel, kinship)
    scale = jnp.sqrt(jnp.float32(gathered.shape[1]))
    kin_panel_t = sent_and_summed(partial_value, COLS, 1)
    total = over_axes(contract(panel_t, kin_panel_t), (("rows_0", "rows_1"), ("cols_0", "cols_1")))
    return (kin_panel_t, total / scale)


def solution(mesh):
    torus = Mesh(mesh.devices.reshape(8, 4, 4, 2), ("rows_0", "rows_1", "cols_0", "cols_1"))
    return jax.shard_map(
        shards,
        mesh=torus,
        in_specs=(P(None, ROWS_COLS), P(ROWS, COLS)),
        out_specs=(P(None, ROWS_COLS), P()),
        check_vma=False,
    )
```

profile of v0, /device:TPU:1, one launch (start us, length us, event | category | flops | bytes accessed | tf_op | source)
XLA Modules:
  0.0 90.5 jit_solution(1889644508145515311)
XLA Ops:
  0.6 0.7 broadcast_in_dim.12
  1.3 0.2 reshape.16
  1.5 21.0 %all_to_all.25 = f32[32,1,1024]{2,1,0:T(1,128)S(1)} all-to-all(f32[32,1,1024]{2,1,0:T(1,128)S(1)} %reshape.16), channel_id=1, replica_groups=mesh['rows_0'=8,'rows_1'=4,'cols_0'=4,'cols_1'=2] {'rows_0','rows_1'}, dimensions={0} | all-to-all | bytes 262144 | tf_op jit(solution)/shard_map/all_to_all | solution.py:14
  22.5 0.5 broadcast.1
  23.0 0.9 %reduce = f32[32,1024]{1,0:T(8,128)S(1)} reduce(f32[32,1,1024]{2,1,0:T(1,128)S(1)} %all_to_all.25, f32[]{:T(128)} %broadcast.1), dimensions={1}, to_apply=%all_to_all.15.reduce_sub_computation | reduce | bytes 262148 | tf_op jit(solution)/shard_map/all_to_all | solution.py:14
  24.0 0.1 reshape.17
  24.1 0.2 broadcast_in_dim.13
  24.3 2.1 %reshape.18 = f32[8,1,32768]{2,1,0:T(1,128)} reshape(f32[8,32,16,64]{3,2,1,0:T(8,128)S(1)} %broadcast_in_dim.13) | data formatting | bytes 2097152
  26.4 6.5 %all-to-all-start.1 = ((f32[8,1,32768]{2,1,0:T(1,128)}), f32[8,1,32768]{2,1,0:T(1,128)S(1)}, u32[]{:S(2)}, u32[]{:S(2)}) async-start(f32[8,1,32768]{2,1,0:T(1,128)} %reshape.18), calls=%async_computation.1 | async-start | bytes 2097152 | tf_op jit(solution)/shard_map/all_to_all | solution.py:14
  33.0 15.0 %all-to-all-done.1 = f32[8,1,32768]{2,1,0:T(1,128)S(1)} async-done(((f32[8,1,32768]{2,1,0:T(1,128)}), f32[8,1,32768]{2,1,0:T(1,128)S(1)}, u32[]{:S(2)}, u32[]{:S(2)}) %all-to-all-start.1) | async-done | bytes 1048608 | tf_op jit(solution)/shard_map/all_to_all | solution.py:14
  47.9 3.1 %reduce.1 = f32[8,32768]{1,0:T(8,128)S(1)} reduce(f32[8,1,32768]{2,1,0:T(1,128)S(1)} %all-to-all-done.1, f32[]{:T(128)} %broadcast.1), dimensions={1}, to_apply=%all_to_all.16.reduce_sub_computation | reduce | bytes 2097156 | tf_op jit(solution)/shard_map/all_to_all | solution.py:14
  51.1 0.8 reshape.19
  51.9 0.2 copy.15
  52.1 0.7 copy.16
  52.8 0.0 copy-start
  52.8 0.7 reshape.14
  53.5 5.7 %fusion = f32[16,512]{1,0:T(8,128)S(1)} fusion(f32[512,2048]{1,0:T(8,128)} %param.3, f32[16,16384]{1,0:T(8,128)S(1)} %reshape.14, s32[]{:T(128)S(6)} %select_n.3), kind=kOutput, calls=%fused_computation.1 | convolution fusion | flops 201326592 | bytes 4358148 | tf_op jit(solution)/shard_map/dot_general | solution.py:52
  59.2 0.1 reshape.15
  59.3 0.1 reshape.20
  59.4 8.1 %all_to_all.26 = f32[8,1,1024]{2,1,0:T(1,128)S(1)} all-to-all(f32[8,1,1024]{2,1,0:T(1,128)S(1)} %reshape.20), channel_id=1, replica_groups=mesh['rows_0'=8,'rows_1'=4,'cols_0'=4,'cols_1'=2] {'cols_0','cols_1'}, dimensions={0} | all-to-all | bytes 65536 | tf_op jit(solution)/shard_map/all_to_all | solution.py:38
  67.4 0.7 reduce.2
  68.2 0.1 reshape.21
  68.3 0.0 copy-done
  68.3 0.0 copy-start.1
  68.3 0.1 convolution_bitcast_fusion
  68.4 0.1 copy.18
  68.5 0.1 reshape.22
  68.6 7.7 %all_to_all.27 = f32[8,1,256]{2,1,0:T(1,128)S(1)} all-to-all(f32[8,1,256]{2,1,0:T(1,128)S(1)} %reshape.22), channel_id=1, replica_groups=mesh['rows_0'=8,'rows_1'=4,'cols_0'=4,'cols_1'=2] {'cols_0','cols_1'}, dimensions={0} | all-to-all | bytes 16384 | tf_op jit(solution)/shard_map/all_to_all | solution.py:14
  76.3 0.7 reduce.3
  77.0 0.1 reshape.23
  77.1 0.1 reshape.24
  77.3 11.8 %all_to_all.28 = f32[32,1,256]{2,1,0:T(1,128)S(1)} all-to-all(f32[32,1,256]{2,1,0:T(1,128)S(1)} %reshape.24), channel_id=1, replica_groups=mesh['rows_0'=8,'rows_1'=4,'cols_0'=4,'cols_1'=2] {'rows_0','rows_1'}, dimensions={0} | all-to-all | bytes 65536 | tf_op jit(solution)/shard_map/all_to_all | solution.py:14
  89.0 0.7 reduce.4
  89.7 0.1 reshape.25
  89.9 0.6 broadcast_multiply_fusion
  90.5 0.0 copy-done.1
  (6 shorter events, 0.1 us)
Async XLA Ops:
  26.4 21.5 %all-to-all-start.1 = ((f32[8,1,32768]{2,1,0:T(1,128)}), f32[8,1,32768]{2,1,0:T(1,128)S(1)}, u32[]{:S(2)}, u32[]{:S(2)}) async-start(f32[8,1,32768]{2,1,0:T(1,128)} %reshape.18), calls=%async_computation.1 | async-start | bytes 2097152 | tf_op jit(solution)/shard_map/all_to_all | solution.py:14
  52.8 15.4 %copy-start = (f32[16,64]{1,0:T(8,128)S(1)}, f32[16,64]{1,0:T(8,128)}, u32[]{:S(2)}) copy-start(f32[16,64]{1,0:T(8,128)} %param.2) | copy-start | bytes 12292
  68.3 22.2 %copy-start.1 = (f32[16,64]{1,0:T(8,128)}, f32[16,64]{1,0:T(8,128)S(1)}, u32[]{:S(2)}) copy-start(f32[16,64]{1,0:T(8,128)S(1)} %reduce_sum.27) | copy-start | bytes 12292
where the time goes:
time: 90.9 us; the launch traced here: 90.5 us
  blocking collectives  48.5 us (53%)
  waiting for transfers between devices  15 us (17%)
  local copies, waits for them, and re-layouts  7.06 us (8%)
  other arithmetic  6.86 us (8%)
  starting transfers between devices  6.53 us (7%)
  matrix products  5.79 us (6%)
    all_to_all x3, blocking collectives, sent_to_all(): return lax.all_to_all(copies, axis, split_axis=0, concat_axis=0, tiled=True)  40.5 us
    all_to_all x1, waiting for transfers between devices, sent_to_all(): return lax.all_to_all(copies, axis, split_axis=0, concat_axis=0, tiled=True)  15 us
    all_to_all x1, blocking collectives, sent_and_summed(): tiles = lax.all_to_all(cut_along(x, dim, length), axis, 0, 0, tiled=True)  8.05 us
    all_to_all x1, starting transfers between devices, sent_to_all(): return lax.all_to_all(copies, axis, split_axis=0, concat_axis=0, tiled=True)  6.53 us
    dot_general x2, matrix products, contract(): lax.dot_general(left, right, (((1,), (1,)), ((), ())), precision=lax.Prec...  5.79 us
    all_to_all x4, other arithmetic, sent_to_all(): return lax.all_to_all(copies, axis, split_axis=0, concat_axis=0, tiled=True)  5.47 us
    unnamed x14, local copies, waits for them, and re-layouts  3.89 us
  transfers between devices with their start and end apart: 1, of which 1 were waited for; matrix products, arithmetic and copies ran while one was open for 0% of the time, Pallas kernels for 0%

commit v1 on v0

v1 whole, which is shorter than its diff:
```python
import itertools

import jax
import jax.numpy as jnp
from jax import lax
from jax.experimental import pallas as pl
from jax.experimental.pallas import tpu as pltpu
from jax.sharding import Mesh
from jax.sharding import PartitionSpec as P

Z, X, Y, C = 8, 4, 4, 2
AXES = ("z", "x", "y", "c")
ROWS = ("z", "x")
COLS = ("y", "c")
PLANE = ("x", "y", "c")
TRAITS = 16
OWN = 64
CHUNKS = 8
HALF = 64
VMEM = pl.BlockSpec(memory_space=pltpu.VMEM)
SMALL = pltpu.CompilerParams(vmem_limit_bytes=2 << 20)
LARGE = pltpu.CompilerParams(vmem_limit_bytes=16 << 20)


def number(z, x, y, c):
    return ((z * X + x) * Y + y) * C + c


def apart(a, b, n):
    d = abs(a - b) % n
    return min(d, n - d)


def plane_to_column():
    pairs = []
    for plane in range(Z):
        y_to, c_to = divmod(plane, C)
        senders = sorted(itertools.product(range(Y), range(C)), key=lambda s: (-apart(s[0], y_to, Y), (s[0] - y_to) % Y, s[1] != c_to))
        planes = sorted(range(Z), key=lambda z: (apart(z, plane, Z), (z - plane) % Z))
        for x in range(X):
            for (y, c), z in zip(senders, planes):
                pairs.append((number(plane, x, y, c), number(z, x, y_to, c_to)))
    return pairs


def low_lanes(shape):
    return lax.broadcasted_iota(jnp.int32, shape, len(shape) - 1) < HALF


def unpacked(a, b):
    low = low_lanes(a.shape)
    top = jnp.where(low, a, pltpu.roll(b, HALF, 1))
    bottom = jnp.where(low, pltpu.roll(a, HALF, 1), b)
    return jnp.concatenate([top, bottom], axis=0)


def packed(tile):
    top, bottom = tile[:8], tile[8:]
    low = low_lanes(top.shape)
    return jnp.where(low, top, pltpu.roll(bottom, HALF, 1)), jnp.where(low, pltpu.roll(top, HALF, 1), bottom)


def split(x):
    high = x.astype(jnp.bfloat16)
    return high, (x - high.astype(jnp.float32)).astype(jnp.bfloat16)


def nt(left, right):
    return lax.dot_general(left, right, (((1,), (1,)), ((), ())), preferred_element_type=jnp.float32)


def nn(left, right):
    return lax.dot_general(left, right, (((1,), (0,)), ((), ())), preferred_element_type=jnp.float32)


def pack_kernel(panel_ref, out_ref):
    panel = panel_ref[...]
    piece = jnp.concatenate([panel[:8], panel[8:]], axis=1)
    out_ref[...] = jnp.broadcast_to(piece[None], out_ref.shape)


def prepare_kernel(x_ref, slab_ref, kinship_ref, high_ref, low_ref, buffer, sems):
    rows = kinship_ref.shape[0]
    height = rows // CHUNKS

    def copy(i):
        return pltpu.make_async_copy(kinship_ref.at[pl.ds(i * height, height)], buffer.at[i], sems.at[i])

    for i in range(CHUNKS):
        copy(i).start()
    start = x_ref[0] * (Y * C)
    own = jnp.concatenate([unpacked(slab_ref[start + j], slab_ref[start + j + 1]) for j in range(0, Y * C, 2)], axis=1)
    own = jnp.concatenate(split(own), axis=0)
    for i in range(CHUNKS):
        copy(i).wait()
        high, low = split(buffer[i])
        high_ref[pl.ds(i * height, height), :] = high
        low_ref[pl.ds(i * height, height), :] = low
    form = nn(own, high_ref[:rows, :]) + nn(own, low_ref[:rows, :])
    high, low = split(form[:TRAITS] + form[TRAITS:])
    high_ref[rows:, :] = jnp.concatenate([high] * 8, axis=0)
    low_ref[rows:, :] = jnp.concatenate([low] * 8, axis=0)


def product_kernel(block_ref, high_ref, low_ref, out_ref):
    columns = high_ref.shape[1]
    tiles = [unpacked(block_ref[j], block_ref[j + 1]) for j in range(0, columns // OWN, 2)]
    panel = jnp.concatenate(split(jnp.concatenate(tiles, axis=1)), axis=0)
    total = nt(panel, high_ref[...]) + nt(panel, low_ref[...])
    total = total[:TRAITS] + total[TRAITS:]
    wide = total[:, -128:]
    row = lax.broadcasted_iota(jnp.int32, wide.shape, 0) % 8
    lane = lax.broadcasted_iota(jnp.int32, wide.shape, 1) // TRAITS
    wide = jnp.where(row == lane, wide, 0.0)
    top = jnp.sum(wide[:8], axis=0, keepdims=True)
    bottom = jnp.sum(wide[8:], axis=0, keepdims=True)
    score = jnp.concatenate([top, bottom, jnp.zeros((6, 128), jnp.float32)], axis=0)
    for y in range(Y):
        pair = packed(total[:, y * 128 : (y + 1) * 128])
        for c in range(C):
            out_ref[y * C + c, :8, :] = pair[c]
            out_ref[y * C + c, 8:, :] = score


def own_kernel(parts_ref, kin_ref, score_ref):
    total = jnp.sum(parts_ref[...], axis=0)
    both = total[:8]
    kin_ref[:8, :] = both[:, :HALF]
    kin_ref[8:, :] = pltpu.roll(both, HALF, 1)[:, :HALF]
    score_ref[...] = jnp.broadcast_to(total[8:10][None], score_ref.shape)


def score_kernel(parts_ref, out_ref, *, scale):
    total = jnp.sum(parts_ref[...], axis=0)
    rows = [total[b // 8 : b // 8 + 1, b % 8 * TRAITS : (b % 8 + 1) * TRAITS] for b in range(TRAITS)]
    out_ref[...] = jnp.concatenate(rows, axis=0).T * scale


def shards(panel_t, kinship):
    f32 = jnp.float32
    slab_rows = kinship.shape[0]
    peers = X * Y * C
    pieces = pl.pallas_call(pack_kernel, out_shape=jax.ShapeDtypeStruct((peers, 8, 128), f32), in_specs=[VMEM], out_specs=VMEM, compiler_params=SMALL, name="pack")(panel_t)
    slab = lax.all_to_all(pieces, PLANE, 0, 0, tiled=True)
    block = lax.ppermute(slab, AXES, plane_to_column())
    x_index = lax.axis_index("x").reshape(1)
    extended = jax.ShapeDtypeStruct((slab_rows + 8 * TRAITS, kinship.shape[1]), jnp.bfloat16)
    high, low = pl.pallas_call(
        prepare_kernel,
        out_shape=(extended, extended),
        in_specs=[pl.BlockSpec(memory_space=pltpu.SMEM), VMEM, pl.BlockSpec(memory_space=pltpu.HBM)],
        out_specs=(VMEM, VMEM),
        scratch_shapes=[pltpu.VMEM((CHUNKS, slab_rows // CHUNKS, kinship.shape[1]), f32), pltpu.SemaphoreType.DMA((CHUNKS,))],
        compiler_params=LARGE,
        name="prepare",
    )(x_index, slab, kinship)
    parts = pl.pallas_call(
        product_kernel,
        out_shape=jax.ShapeDtypeStruct((Y * C, 16, 128), f32),
        in_specs=[VMEM, VMEM, VMEM],
        out_specs=VMEM,
        compiler_params=LARGE,
        name="product",
    )(block, high, low)
    parts = lax.all_to_all(parts, COLS, 0, 0, tiled=True)
    kin_panel_t, scores = pl.pallas_call(
        own_kernel,
        out_shape=(jax.ShapeDtypeStruct(panel_t.shape, f32), jax.ShapeDtypeStruct((Z * X, 2, 128), f32)),
        in_specs=[VMEM],
        out_specs=(VMEM, VMEM),
        compiler_params=SMALL,
        name="own",
    )(parts)
    scores = lax.all_to_all(scores, ROWS, 0, 0, tiled=True)
    samples = OWN * Z * X * Y * C
    score = pl.pallas_call(
        lambda parts_ref, out_ref: score_kernel(parts_ref, out_ref, scale=samples**-0.5),
        out_shape=jax.ShapeDtypeStruct((TRAITS, TRAITS), f32),
        in_specs=[VMEM],
        out_specs=VMEM,
        compiler_params=SMALL,
        name="score",
    )(scores)
    return kin_panel_t, score


def solution(mesh):
    torus = Mesh(mesh.devices.reshape(Z, X, Y, C), AXES)
    return jax.shard_map(
        shards,
        mesh=torus,
        in_specs=(P(None, AXES), P(ROWS, COLS)),
        out_specs=(P(None, AXES), P()),
        check_vma=False,
    )
```

time: 90.9 us -> 56.1 us (0.62)
  waiting for transfers between devices: 15 us -> 0.01 us
  blocking collectives: 48.5 us -> 40 us
  other arithmetic: 6.86 us -> 0 us
  matrix products: 5.79 us -> 0 us
  Pallas kernels: 0 us -> 5.06 us
  local copies, waits for them, and re-layouts: 7.06 us -> 2.88 us
    all_to_all x1 -> x0, waiting for transfers between devices: 15 us -> none  [sent_to_all(): return lax.all_to_all(copies, axis, split_axis=0, concat_axis=0, tiled=True)]
    all_to_all x4 -> x3, blocking collectives: 48.5 us -> 40 us  [the longest x1 16 us: shards(): slab = lax.all_to_all(pieces, PLANE, 0, 0, tiled=True)]
    ppermute x0 -> x1, starting transfers between devices: none -> 7.19 us  [shards(): block = lax.ppermute(slab, AXES, plane_to_column())]
    all_to_all x1 -> x0, starting transfers between devices: 6.53 us -> none  [sent_to_all(): return lax.all_to_all(copies, axis, split_axis=0, concat_axis=0, tiled=True)]
    all_to_all x5 -> x0, other arithmetic: 6.19 us -> none  [the longest x4 5.47 us: sent_to_all(): return lax.all_to_all(copies, axis, split_axis=0, concat_axis=0, tiled=True)]
    dot_general x2 -> x0, matrix products: 5.79 us -> none  [contract(): lax.dot_general(left, right, (((1,), (1,)), ((), ())), precision=lax.Prec...]
    pallas_call x0 -> x5, Pallas kernels: none -> 5.06 us  [the longest x1 1.93 us: shards(): pl.pallas_call(prepare_kernel, out_shape=(extended, extended), in_specs=[...]
    unnamed x14 -> x4, local copies, waits for them, and re-layouts: 3.89 us -> 2.88 us
  transfers between devices with their start and end apart: 1 -> 1, of which waited for: 1 -> 0; matrix products, arithmetic and copies ran while one was open for 0% -> 0% of each run, Pallas kernels for 0% -> 3%
where the time goes in v1:
time: 56.1 us; the launch traced here: 55.8 us
  blocking collectives  40 us (71%)
  starting transfers between devices  7.19 us (13%)
  Pallas kernels  5.06 us (9%)
  local copies, waits for them, and re-layouts  2.88 us (5%)
  between operations  0.66 us (1%)
    all_to_all x1, blocking collectives, shards(): slab = lax.all_to_all(pieces, PLANE, 0, 0, tiled=True)  16 us
    all_to_all x1, blocking collectives, shards(): scores = lax.all_to_all(scores, ROWS, 0, 0, tiled=True)  15.9 us
    all_to_all x1, blocking collectives, shards(): parts = lax.all_to_all(parts, COLS, 0, 0, tiled=True)  8.1 us
    ppermute x1, starting transfers between devices, shards(): block = lax.ppermute(slab, AXES, plane_to_column())  7.19 us
    unnamed x4, local copies, waits for them, and re-layouts  2.88 us
    pallas_call x1, Pallas kernels, shards(): pl.pallas_call(prepare_kernel, out_shape=(extended, extended), in_specs=[...  1.93 us
    pallas_call x1, Pallas kernels, shards(): pl.pallas_call(product_kernel, out_shape=jax.ShapeDtypeStruct((Y * C, 16,...  1.6 us
  transfers between devices with their start and end apart: 1, of which 0 were waited for; matrix products, arithmetic and copies ran while one was open for 0% of the time, Pallas kernels for 3%

profile of v1, /device:TPU:1, one launch (start us, length us, event | category | flops | bytes accessed | tf_op | source)
XLA Modules:
  0.0 55.8 jit_solution(3804611324748740334)
XLA Ops:
  0.6 0.0 copy-start.1
  0.6 0.7 %copy-done.1 = f32[16,64]{1,0:T(8,128)S(1)} copy-done((f32[16,64]{1,0:T(8,128)S(1)}, f32[16,64]{1,0:T(8,128)}, u32[]{:S(2)}) %copy-start.1) | copy-done | bytes 4120
  1.3 0.1 pack.1
  1.4 16.0 %all_to_all.15.slab_ref = f32[32,8,128]{2,1,0:T(8,128)S(1)} all-to-all(f32[32,8,128]{2,1,0:T(8,128)S(1)} %pack.1), channel_id=1, replica_groups=mesh['z'=8,'x'=4,'y'=4,'c'=2] {'x','y','c'}, dimensions={0} | all-to-all | bytes 262144 | tf_op jit(solution)/shard_map/all_to_all | solution.py:144
  17.5 7.2 %collective-permute-start = (f32[32,8,128]{2,1,0:T(8,128)S(1)}, f32[32,8,128]{2,1,0:T(8,128)S(1)}, u32[]{:S(2)}, u32[]{:S(2)}) collective-permute-start(f32[32,8,128]{2,1,0:T(8,128)S(1)} %all_to_all.15.slab_ref), channel_id=1, source_target_pairs={{4,0},{5,32},{2,224},{3,64},{6,192},{7,96},{0,160},{1,128},{12,8},... | collective-permute-start | bytes 393224 | tf_op jit(solution)/shard_map/ppermute | solution.py:145
  24.6 0.0 copy-start
  24.6 2.2 %copy-done = f32[512,2048]{1,0:T(8,128)S(1)} copy-done((f32[512,2048]{1,0:T(8,128)S(1)}, f32[512,2048]{1,0:T(8,128)}, u32[]{:S(2)}) %copy-start) | copy-done | bytes 4194328
  26.8 1.9 %prepare.1 = (bf16[640,2048]{1,0:T(8,128)(2,1)S(1)}, bf16[640,2048]{1,0:T(8,128)(2,1)S(1)}) custom-call(s32[1]{0:T(128)} %bitcast.x_ref, f32[32,8,128]{2,1,0:T(8,128)S(1)} %all_to_all.15.slab_ref, f32[512,2048]{1,0:T(8,128)S(1)} %copy-done), custom_call_target="tpu_custom_call" | custom-call | tf_op jit(solution)/shard_map/prepare/pallas_call | solution.py:148
  28.8 0.0 collective-permute-done.block_ref
  28.8 1.6 %product.1 = f32[8,16,128]{2,1,0:T(8,128)S(1)} custom-call(f32[32,8,128]{2,1,0:T(8,128)S(1)} %collective-permute-done.block_ref, bf16[640,2048]{1,0:T(8,128)(2,1)S(1)} %get-tuple-element.6.high_ref, bf16[640,2048]{1,0:T(8,128)(2,1)S(1)} %get-tuple-element.7.low_ref), custom_call_target="tpu_custom_call" | custom-call | tf_op jit(solution)/shard_map/product/pallas_call | solution.py:157
  30.4 8.1 %all_to_all.16.parts_ref = f32[8,16,128]{2,1,0:T(8,128)S(1)} all-to-all(f32[8,16,128]{2,1,0:T(8,128)S(1)} %product.1), channel_id=1, replica_groups=mesh['z'=8,'x'=4,'y'=4,'c'=2] {'y','c'}, dimensions={0} | all-to-all | bytes 131072 | tf_op jit(solution)/shard_map/all_to_all | solution.py:165
  38.5 0.7 %own.1 = (f32[16,64]{1,0:T(8,128)}, f32[32,2,128]{2,1,0:T(2,128)S(1)}) custom-call(f32[8,16,128]{2,1,0:T(8,128)S(1)} %all_to_all.16.parts_ref), custom_call_target="tpu_custom_call" | custom-call | tf_op jit(solution)/shard_map/own/pallas_call | solution.py:166
  39.2 15.9 %all_to_all.17.parts_ref = f32[32,2,128]{2,1,0:T(2,128)S(1)} all-to-all(f32[32,2,128]{2,1,0:T(2,128)S(1)} %get-tuple-element.9), channel_id=1, replica_groups=mesh['z'=8,'x'=4,'y'=4,'c'=2] {'z','x'}, dimensions={0} | all-to-all | bytes 65536 | tf_op jit(solution)/shard_map/all_to_all | solution.py:174
  55.0 0.8 %score.1 = f32[16,16]{1,0:T(8,128)} custom-call(f32[32,2,128]{2,1,0:T(2,128)S(1)} %all_to_all.17.parts_ref), custom_call_target="tpu_custom_call" | custom-call | tf_op jit(solution)/shard_map/score/pallas_call | solution.py:176
Async XLA Ops:
  0.6 0.7 %copy-start.1 = (f32[16,64]{1,0:T(8,128)S(1)}, f32[16,64]{1,0:T(8,128)}, u32[]{:S(2)}) copy-start(f32[16,64]{1,0:T(8,128)} %panel_ref.1) | copy-start | bytes 12292
  17.5 11.3 %collective-permute-start = (f32[32,8,128]{2,1,0:T(8,128)S(1)}, f32[32,8,128]{2,1,0:T(8,128)S(1)}, u32[]{:S(2)}, u32[]{:S(2)}) collective-permute-start(f32[32,8,128]{2,1,0:T(8,128)S(1)} %all_to_all.15.slab_ref), channel_id=1, source_target_pairs={{4,0},{5,32},{2,224},{3,64},{6,192},{7,96},{0,160},{1,128},{12,8},... | collective-permute-start | bytes 393224 | tf_op jit(solution)/shard_map/ppermute | solution.py:145
  24.6 2.2 %copy-start = (f32[512,2048]{1,0:T(8,128)S(1)}, f32[512,2048]{1,0:T(8,128)}, u32[]{:S(2)}) copy-start(f32[512,2048]{1,0:T(8,128)} %kinship_ref.1) | copy-start | bytes 12582916

commit v2 on v1

--- a/solution.py
+++ b/solution.py
@@ -20,6 +20,7 @@
 VMEM = pl.BlockSpec(memory_space=pltpu.VMEM)
 SMALL = pltpu.CompilerParams(vmem_limit_bytes=2 << 20)
 LARGE = pltpu.CompilerParams(vmem_limit_bytes=16 << 20)
+WHOLE = pltpu.CompilerParams(vmem_limit_bytes=48 << 20)
 
 
 def number(z, x, y, c):
@@ -98,17 +99,19 @@
         low_ref[pl.ds(i * height, height), :] = low
     form = nn(own, high_ref[:rows, :]) + nn(own, low_ref[:rows, :])
     high, low = split(form[:TRAITS] + form[TRAITS:])
-    high_ref[rows:, :] = jnp.concatenate([high] * 8, axis=0)
-    low_ref[rows:, :] = jnp.concatenate([low] * 8, axis=0)
+    high_ref[rows:, :] = jnp.concatenate([high] * 4 + [low] * 4, axis=0)
 
 
 def product_kernel(block_ref, high_ref, low_ref, out_ref):
     columns = high_ref.shape[1]
     tiles = [unpacked(block_ref[j], block_ref[j + 1]) for j in range(0, columns // OWN, 2)]
     panel = jnp.concatenate(split(jnp.concatenate(tiles, axis=1)), axis=0)
-    total = nt(panel, high_ref[...]) + nt(panel, low_ref[...])
+    rows = low_ref.shape[0]
+    first = nt(panel, high_ref[...])
+    total = first[:, :rows] + nt(panel, low_ref[...])
     total = total[:TRAITS] + total[TRAITS:]
-    wide = total[:, -128:]
+    wide = first[:TRAITS, rows:] + first[TRAITS:, rows:]
+    wide = wide + pltpu.roll(wide, HALF, 1)
     row = lax.broadcasted_iota(jnp.int32, wide.shape, 0) % 8
     lane = lax.broadcasted_iota(jnp.int32, wide.shape, 1) // TRAITS
     wide = jnp.where(row == lane, wide, 0.0)
@@ -122,18 +125,19 @@
             out_ref[y * C + c, 8:, :] = score
 
 
-def own_kernel(parts_ref, kin_ref, score_ref):
+def own_kernel(parts_ref, own_ref, score_ref):
     total = jnp.sum(parts_ref[...], axis=0)
-    both = total[:8]
-    kin_ref[:8, :] = both[:, :HALF]
-    kin_ref[8:, :] = pltpu.roll(both, HALF, 1)[:, :HALF]
+    own_ref[...] = total[:8]
     score_ref[...] = jnp.broadcast_to(total[8:10][None], score_ref.shape)
 
 
-def score_kernel(parts_ref, out_ref, *, scale):
+def result_kernel(own_ref, parts_ref, kin_ref, score_ref, *, scale):
+    own = own_ref[...]
+    kin_ref[:8, :] = own[:, :HALF]
+    kin_ref[8:, :] = pltpu.roll(own, HALF, 1)[:, :HALF]
     total = jnp.sum(parts_ref[...], axis=0)
     rows = [total[b // 8 : b // 8 + 1, b % 8 * TRAITS : (b % 8 + 1) * TRAITS] for b in range(TRAITS)]
-    out_ref[...] = jnp.concatenate(rows, axis=0).T * scale
+    score_ref[...] = jnp.concatenate(rows, axis=0).T * scale
 
 
 def shards(panel_t, kinship):
@@ -144,14 +148,16 @@
     slab = lax.all_to_all(pieces, PLANE, 0, 0, tiled=True)
     block = lax.ppermute(slab, AXES, plane_to_column())
     x_index = lax.axis_index("x").reshape(1)
-    extended = jax.ShapeDtypeStruct((slab_rows + 8 * TRAITS, kinship.shape[1]), jnp.bfloat16)
     high, low = pl.pallas_call(
         prepare_kernel,
-        out_shape=(extended, extended),
+        out_shape=(
+            jax.ShapeDtypeStruct((slab_rows + 8 * TRAITS, kinship.shape[1]), jnp.bfloat16),
+            jax.ShapeDtypeStruct(kinship.shape, jnp.bfloat16),
+        ),
         in_specs=[pl.BlockSpec(memory_space=pltpu.SMEM), VMEM, pl.BlockSpec(memory_space=pltpu.HBM)],
         out_specs=(VMEM, VMEM),
         scratch_shapes=[pltpu.VMEM((CHUNKS, slab_rows // CHUNKS, kinship.shape[1]), f32), pltpu.SemaphoreType.DMA((CHUNKS,))],
-        compiler_params=LARGE,
+        compiler_params=WHOLE,
         name="prepare",
     )(x_index, slab, kinship)
     parts = pl.pallas_call(
@@ -163,9 +169,9 @@
         name="product",
     )(block, high, low)
     parts = lax.all_to_all(parts, COLS, 0, 0, tiled=True)
-    kin_panel_t, scores = pl.pallas_call(
+    own, scores = pl.pallas_call(
         own_kernel,
-        out_shape=(jax.ShapeDtypeStruct(panel_t.shape, f32), jax.ShapeDtypeStruct((Z * X, 2, 128), f32)),
+        out_shape=(jax.ShapeDtypeStruct((8, 128), f32), jax.ShapeDtypeStruct((Z * X, 2, 128), f32)),
         in_specs=[VMEM],
         out_specs=(VMEM, VMEM),
         compiler_params=SMALL,
@@ -173,15 +179,14 @@
     )(parts)
     scores = lax.all_to_all(scores, ROWS, 0, 0, tiled=True)
     samples = OWN * Z * X * Y * C
-    score = pl.pallas_call(
-        lambda parts_ref, out_ref: score_kernel(parts_ref, out_ref, scale=samples**-0.5),
-        out_shape=jax.ShapeDtypeStruct((TRAITS, TRAITS), f32),
-        in_specs=[VMEM],
-        out_specs=VMEM,
+    return pl.pallas_call(
+        lambda *refs: result_kernel(*refs, scale=samples**-0.5),
+        out_shape=(jax.ShapeDtypeStruct(panel_t.shape, f32), jax.ShapeDtypeStruct((TRAITS, TRAITS), f32)),
+        in_specs=[VMEM, VMEM],
+        out_specs=(VMEM, VMEM),
         compiler_params=SMALL,
-        name="score",
-    )(scores)
-    return kin_panel_t, score
+        name="result",
+    )(own, scores)
 
 
 def solution(mesh):

time: 56.1 us -> 55.3 us (0.986)
  local copies, waits for them, and re-layouts: 2.88 us -> 0.69 us
  blocking collectives: 40 us -> 41 us
    unnamed x4 -> x2, local copies, waits for them, and re-layouts: 2.88 us -> 0.69 us
    all_to_all x1, blocking collectives: 8.1 us -> 8.86 us  [shards(): parts = lax.all_to_all(parts, COLS, 0, 0, tiled=True)]
  transfers between devices with their start and end apart: 1 -> 1, of which waited for: 0 -> 1; matrix products, arithmetic and copies ran while one was open for 0% -> 0% of each run, Pallas kernels for 3% -> 6%
where the time goes in v2:
time: 55.3 us; the launch traced here: 55.1 us
  blocking collectives  41 us (74%)
  starting transfers between devices  7.19 us (13%)
  Pallas kernels  5.38 us (10%)
  local copies, waits for them, and re-layouts  0.69 us (1%)
  between operations  0.65 us (1%)
    all_to_all x1, blocking collectives, shards(): scores = lax.all_to_all(scores, ROWS, 0, 0, tiled=True)  16.1 us
    all_to_all x1, blocking collectives, shards(): slab = lax.all_to_all(pieces, PLANE, 0, 0, tiled=True)  16 us
    all_to_all x1, blocking collectives, shards(): parts = lax.all_to_all(parts, COLS, 0, 0, tiled=True)  8.86 us
    ppermute x1, starting transfers between devices, shards(): block = lax.ppermute(slab, AXES, plane_to_column())  7.19 us
    pallas_call x1, Pallas kernels, shards(): pl.pallas_call(prepare_kernel, out_shape=(jax.ShapeDtypeStruct((slab_rows...  3.03 us
    pallas_call x1, Pallas kernels, shards(): pl.pallas_call(product_kernel, out_shape=jax.ShapeDtypeStruct((Y * C, 16,...  1.46 us
  transfers between devices with their start and end apart: 1, of which 1 were waited for; matrix products, arithmetic and copies ran while one was open for 0% of the time, Pallas kernels for 6%

profile of v2, /device:TPU:1, one launch (start us, length us, event | category | flops | bytes accessed | tf_op | source)
XLA Modules:
  0.0 55.1 jit_solution(3360231249306442683)
XLA Ops:
  0.6 0.0 copy-start
  0.6 0.7 %copy-done = f32[16,64]{1,0:T(8,128)S(1)} copy-done((f32[16,64]{1,0:T(8,128)S(1)}, f32[16,64]{1,0:T(8,128)}, u32[]{:S(2)}) %copy-start) | copy-done | bytes 4120
  1.3 0.1 pack.1
  1.4 16.0 %all_to_all.15.slab_ref = f32[32,8,128]{2,1,0:T(8,128)S(1)} all-to-all(f32[32,8,128]{2,1,0:T(8,128)S(1)} %pack.1), channel_id=1, replica_groups=mesh['z'=8,'x'=4,'y'=4,'c'=2] {'x','y','c'}, dimensions={0} | all-to-all | bytes 262144 | tf_op jit(solution)/shard_map/all_to_all | solution.py:148
  17.5 7.2 %collective-permute-start = (f32[32,8,128]{2,1,0:T(8,128)S(1)}, f32[32,8,128]{2,1,0:T(8,128)S(1)}, u32[]{:S(2)}, u32[]{:S(2)}) collective-permute-start(f32[32,8,128]{2,1,0:T(8,128)S(1)} %all_to_all.15.slab_ref), channel_id=1, source_target_pairs={{4,0},{5,32},{2,224},{3,64},{6,192},{7,96},{0,160},{1,128},{12,8},... | collective-permute-start | bytes 393224 | tf_op jit(solution)/shard_map/ppermute | solution.py:149
  24.6 3.0 %prepare.1 = (bf16[640,2048]{1,0:T(8,128)(2,1)S(1)}, bf16[512,2048]{1,0:T(8,128)(2,1)S(1)}) custom-call(s32[1]{0:T(128)} %bitcast.x_ref, f32[32,8,128]{2,1,0:T(8,128)S(1)} %all_to_all.15.slab_ref, f32[512,2048]{1,0:T(8,128)} %kinship_ref.1), custom_call_target="tpu_custom_call" | custom-call | tf_op jit(solution)/shard_map/prepare/pallas_call | solution.py:151
  27.7 0.2 collective-permute-done.block_ref
  27.9 1.5 %product.1 = f32[8,16,128]{2,1,0:T(8,128)S(1)} custom-call(f32[32,8,128]{2,1,0:T(8,128)S(1)} %collective-permute-done.block_ref, bf16[640,2048]{1,0:T(8,128)(2,1)S(1)} %get-tuple-element.6.high_ref, bf16[512,2048]{1,0:T(8,128)(2,1)S(1)} %get-tuple-element.7.low_ref), custom_call_target="tpu_custom_call" | custom-call | tf_op jit(solution)/shard_map/product/pallas_call | solution.py:163
  29.3 8.9 %all_to_all.16.parts_ref = f32[8,16,128]{2,1,0:T(8,128)S(1)} all-to-all(f32[8,16,128]{2,1,0:T(8,128)S(1)} %product.1), channel_id=1, replica_groups=mesh['z'=8,'x'=4,'y'=4,'c'=2] {'y','c'}, dimensions={0} | all-to-all | bytes 131072 | tf_op jit(solution)/shard_map/all_to_all | solution.py:171
  38.2 16.1 %all_to_all.17.refs_1_ = f32[32,2,128]{2,1,0:T(2,128)S(1)} all-to-all(f32[32,2,128]{2,1,0:T(2,128)S(1)} %get-tuple-element.9), channel_id=1, replica_groups=mesh['z'=8,'x'=4,'y'=4,'c'=2] {'z','x'}, dimensions={0} | all-to-all | bytes 65536 | tf_op jit(solution)/shard_map/all_to_all | solution.py:180
  54.3 0.8 %result.1 = (f32[16,64]{1,0:T(8,128)}, f32[16,16]{1,0:T(8,128)}) custom-call(f32[8,128]{1,0:T(8,128)S(1)} %get-tuple-element.8.refs_0_, f32[32,2,128]{2,1,0:T(2,128)S(1)} %all_to_all.17.refs_1_), custom_call_target="tpu_custom_call" | custom-call | tf_op jit(solution)/shard_map/result/pallas_call | solution.py:182
  (1 shorter events, 0.0 us)
Async XLA Ops:
  0.6 0.7 %copy-start = (f32[16,64]{1,0:T(8,128)S(1)}, f32[16,64]{1,0:T(8,128)}, u32[]{:S(2)}) copy-start(f32[16,64]{1,0:T(8,128)} %panel_ref.1) | copy-start | bytes 12292
  17.5 10.4 %collective-permute-start = (f32[32,8,128]{2,1,0:T(8,128)S(1)}, f32[32,8,128]{2,1,0:T(8,128)S(1)}, u32[]{:S(2)}, u32[]{:S(2)}) collective-permute-start(f32[32,8,128]{2,1,0:T(8,128)S(1)} %all_to_all.15.slab_ref), channel_id=1, source_target_pairs={{4,0},{5,32},{2,224},{3,64},{6,192},{7,96},{0,160},{1,128},{12,8},... | collective-permute-start | bytes 393224 | tf_op jit(solution)/shard_map/ppermute | solution.py:149

commit v3 on v2

--- a/solution.py
+++ b/solution.py
@@ -102,15 +102,24 @@
     high_ref[rows:, :] = jnp.concatenate([high] * 4 + [low] * 4, axis=0)
 
 
-def product_kernel(block_ref, high_ref, low_ref, out_ref):
-    columns = high_ref.shape[1]
-    tiles = [unpacked(block_ref[j], block_ref[j + 1]) for j in range(0, columns // OWN, 2)]
+def half_product(block_ref, high_ref, low_ref, start):
+    columns = block_ref.shape[0] * OWN
+    tiles = [unpacked(block_ref[j], block_ref[j + 1]) for j in range(0, block_ref.shape[0], 2)]
     panel = jnp.concatenate(split(jnp.concatenate(tiles, axis=1)), axis=0)
     rows = low_ref.shape[0]
-    first = nt(panel, high_ref[...])
-    total = first[:, :rows] + nt(panel, low_ref[...])
-    total = total[:TRAITS] + total[TRAITS:]
-    wide = first[:TRAITS, rows:] + first[TRAITS:, rows:]
+    both = nt(panel, high_ref[:, start : start + columns])
+    partial = both[:, :rows] + nt(panel, low_ref[:, start : start + columns])
+    return partial[:TRAITS] + partial[TRAITS:], both[:TRAITS, rows:] + both[TRAITS:, rows:]
+
+
+def first_kernel(block_ref, high_ref, low_ref, partial_ref, wide_ref):
+    partial_ref[...], wide_ref[...] = half_product(block_ref, high_ref, low_ref, 0)
+
+
+def second_kernel(block_ref, high_ref, low_ref, partial_ref, wide_ref, out_ref):
+    total, wide = half_product(block_ref, high_ref, low_ref, block_ref.shape[0] * OWN)
+    total = total + partial_ref[...]
+    wide = wide + wide_ref[...]
     wide = wide + pltpu.roll(wide, HALF, 1)
     row = lax.broadcasted_iota(jnp.int32, wide.shape, 0) % 8
     lane = lax.broadcasted_iota(jnp.int32, wide.shape, 1) // TRAITS
@@ -146,7 +155,9 @@
     peers = X * Y * C
     pieces = pl.pallas_call(pack_kernel, out_shape=jax.ShapeDtypeStruct((peers, 8, 128), f32), in_specs=[VMEM], out_specs=VMEM, compiler_params=SMALL, name="pack")(panel_t)
     slab = lax.all_to_all(pieces, PLANE, 0, 0, tiled=True)
-    block = lax.ppermute(slab, AXES, plane_to_column())
+    pairs = plane_to_column()
+    early = lax.ppermute(slab[: peers // 2], AXES, pairs)
+    late = lax.ppermute(slab[peers // 2 :], AXES, pairs)
     x_index = lax.axis_index("x").reshape(1)
     high, low = pl.pallas_call(
         prepare_kernel,
@@ -160,14 +171,22 @@
         compiler_params=WHOLE,
         name="prepare",
     )(x_index, slab, kinship)
+    partial, wide = pl.pallas_call(
+        first_kernel,
+        out_shape=(jax.ShapeDtypeStruct((TRAITS, slab_rows), f32), jax.ShapeDtypeStruct((TRAITS, 8 * TRAITS), f32)),
+        in_specs=[VMEM, VMEM, VMEM],
+        out_specs=(VMEM, VMEM),
+        compiler_params=LARGE,
+        name="first",
+    )(early, high, low)
     parts = pl.pallas_call(
-        product_kernel,
+        second_kernel,
         out_shape=jax.ShapeDtypeStruct((Y * C, 16, 128), f32),
-        in_specs=[VMEM, VMEM, VMEM],
+        in_specs=[VMEM] * 5,
         out_specs=VMEM,
         compiler_params=LARGE,
-        name="product",
-    )(block, high, low)
+        name="second",
+    )(late, high, low, partial, wide)
     parts = lax.all_to_all(parts, COLS, 0, 0, tiled=True)
     own, scores = pl.pallas_call(
         own_kernel,

time: 55.3 us -> 54.9 us (level)
  blocking collectives: 41 us -> 38.5 us
  starting transfers between devices: 7.19 us -> 8.23 us
  waiting for transfers between devices: 0.18 us -> 1.03 us
    all_to_all x1, blocking collectives: 16.1 us -> 12.1 us  [shards(): scores = lax.all_to_all(scores, ROWS, 0, 0, tiled=True)]
    all_to_all x1, blocking collectives: 8.86 us -> 10.3 us  [shards(): parts = lax.all_to_all(parts, COLS, 0, 0, tiled=True)]
    ppermute x1 -> x2, starting transfers between devices: 7.19 us -> 8.23 us  [the longest x1 7.28 us: shards(): early = lax.ppermute(slab[:peers // 2], AXES, pairs)]
    ppermute x1 -> x2, waiting for transfers between devices: 0.18 us -> 1.03 us  [the longest x1 1.03 us: shards(): late = lax.ppermute(slab[peers // 2:], AXES, pairs)]
    pallas_call x1 -> x2, Pallas kernels: 1.46 us -> 1.61 us  [the longest x1 0.86 us: shards(): pl.pallas_call(second_kernel, out_shape=jax.ShapeDtypeStruct((Y * C, 16,...]
  transfers between devices with their start and end apart: 1 -> 2, of which waited for: 1 -> 1; matrix products, arithmetic and copies ran while one was open for 0% -> 0% of each run, Pallas kernels for 6% -> 7%
where the time goes in v3:
time: 54.9 us; the launch traced here: 54.7 us
  blocking collectives  38.5 us (70%)
  starting transfers between devices  8.23 us (15%)
  Pallas kernels  5.52 us (10%)
  waiting for transfers between devices  1.03 us (2%)
  local copies, waits for them, and re-layouts  0.7 us (1%)
  between operations  0.67 us (1%)
    all_to_all x1, blocking collectives, shards(): slab = lax.all_to_all(pieces, PLANE, 0, 0, tiled=True)  16 us
    all_to_all x1, blocking collectives, shards(): scores = lax.all_to_all(scores, ROWS, 0, 0, tiled=True)  12.1 us
    all_to_all x1, blocking collectives, shards(): parts = lax.all_to_all(parts, COLS, 0, 0, tiled=True)  10.3 us
    ppermute x1, starting transfers between devices, shards(): early = lax.ppermute(slab[:peers // 2], AXES, pairs)  7.28 us
    pallas_call x1, Pallas kernels, shards(): pl.pallas_call(prepare_kernel, out_shape=(jax.ShapeDtypeStruct((slab_rows...  3.03 us
  transfers between devices with their start and end apart: 2, of which 1 were waited for; matrix products, arithmetic and copies ran while one was open for 0% of the time, Pallas kernels for 7%

profile of v3, /device:TPU:1, one launch (start us, length us, event | category | flops | bytes accessed | tf_op | source)
XLA Modules:
  0.0 54.7 jit_solution(375435950939896241)
XLA Ops:
  0.6 0.0 copy-start
  0.6 0.7 %copy-done = f32[16,64]{1,0:T(8,128)S(1)} copy-done((f32[16,64]{1,0:T(8,128)S(1)}, f32[16,64]{1,0:T(8,128)}, u32[]{:S(2)}) %copy-start) | copy-done | bytes 4120
  1.3 0.1 pack.1
  1.4 16.0 %all_to_all.15.slab_ref = f32[32,8,128]{2,1,0:T(8,128)S(1)} all-to-all(f32[32,8,128]{2,1,0:T(8,128)S(1)} %pack.1), channel_id=1, replica_groups=mesh['z'=8,'x'=4,'y'=4,'c'=2] {'x','y','c'}, dimensions={0} | all-to-all | bytes 262144 | tf_op jit(solution)/shard_map/all_to_all | solution.py:157
  17.5 7.3 %collective-permute-start.1 = (f32[16,8,128]{2,1,0:T(8,128)S(1)}, f32[16,8,128]{2,1,0:T(8,128)S(1)}, u32[]{:S(2)}, u32[]{:S(2)}) collective-permute-start(f32[16,8,128]{2,1,0:T(8,128)S(1)} %get-tuple-element.14), channel_id=1, source_target_pairs={{4,0},{5,32},{2,224},{3,64},{6,192},{7,96},{0,160},{1,128},{12,8},... | collective-permute-start | bytes 196616 | tf_op jit(solution)/shard_map/ppermute | solution.py:159
  24.7 1.0 %collective-permute-start = (f32[16,8,128]{2,1,0:T(8,128)S(1)}, f32[16,8,128]{2,1,0:T(8,128)S(1)}, u32[]{:S(2)}, u32[]{:S(2)}) collective-permute-start(f32[16,8,128]{2,1,0:T(8,128)S(1)} %get-tuple-element.15), channel_id=1, source_target_pairs={{4,0},{5,32},{2,224},{3,64},{6,192},{7,96},{0,160},{1,128},{12,8},... | collective-permute-start | bytes 196616 | tf_op jit(solution)/shard_map/ppermute | solution.py:160
  25.7 3.0 %prepare.1 = (bf16[640,2048]{1,0:T(8,128)(2,1)S(1)}, bf16[512,2048]{1,0:T(8,128)(2,1)S(1)}) custom-call(s32[1]{0:T(128)} %bitcast.x_ref, f32[32,8,128]{2,1,0:T(8,128)S(1)} %all_to_all.15.slab_ref, f32[512,2048]{1,0:T(8,128)} %kinship_ref.1), custom_call_target="tpu_custom_call" | custom-call | tf_op jit(solution)/shard_map/prepare/pallas_call | solution.py:162
  28.7 0.0 collective-permute-done.1.block_ref
  28.8 0.8 %first.1 = (f32[16,512]{1,0:T(8,128)S(1)}, f32[16,128]{1,0:T(8,128)S(1)}) custom-call(f32[16,8,128]{2,1,0:T(8,128)S(1)} %collective-permute-done.1.block_ref, bf16[640,2048]{1,0:T(8,128)(2,1)S(1)} %get-tuple-element.8.high_ref, bf16[512,2048]{1,0:T(8,128)(2,1)S(1)} %get-tuple-element.9.low_ref), custom_call_target="tpu_custom_call" | custom-call | tf_op jit(solution)/shard_map/first/pallas_call | solution.py:174
  29.5 1.0 %collective-permute-done.block_ref = f32[16,8,128]{2,1,0:T(8,128)S(1)} collective-permute-done((f32[16,8,128]{2,1,0:T(8,128)S(1)}, f32[16,8,128]{2,1,0:T(8,128)S(1)}, u32[]{:S(2)}, u32[]{:S(2)}) %collective-permute-start) | collective-permute-done | bytes 65568 | tf_op jit(solution)/shard_map/ppermute | solution.py:160
  30.5 0.9 %second.1 = f32[8,16,128]{2,1,0:T(8,128)S(1)} custom-call(f32[16,8,128]{2,1,0:T(8,128)S(1)} %collective-permute-done.block_ref, bf16[640,2048]{1,0:T(8,128)(2,1)S(1)} %get-tuple-element.8.high_ref, bf16[512,2048]{1,0:T(8,128)(2,1)S(1)} %get-tuple-element.9.low_ref, f32[16,512]{1,0:T(8,128)S(1)} %get-tuple-element.10.partial_ref, ...), custom_call_target="tpu_custom_call" | custom-call | tf_op jit(solution)/shard_map/second/pallas_call | solution.py:182
  31.4 10.3 %all_to_all.16.parts_ref = f32[8,16,128]{2,1,0:T(8,128)S(1)} all-to-all(f32[8,16,128]{2,1,0:T(8,128)S(1)} %second.1), channel_id=1, replica_groups=mesh['z'=8,'x'=4,'y'=4,'c'=2] {'y','c'}, dimensions={0} | all-to-all | bytes 131072 | tf_op jit(solution)/shard_map/all_to_all | solution.py:190
  41.7 12.1 %all_to_all.17.refs_1_ = f32[32,2,128]{2,1,0:T(2,128)S(1)} all-to-all(f32[32,2,128]{2,1,0:T(2,128)S(1)} %get-tuple-element.13), channel_id=1, replica_groups=mesh['z'=8,'x'=4,'y'=4,'c'=2] {'z','x'}, dimensions={0} | all-to-all | bytes 65536 | tf_op jit(solution)/shard_map/all_to_all | solution.py:199
  53.9 0.8 %result.1 = (f32[16,64]{1,0:T(8,128)}, f32[16,16]{1,0:T(8,128)}) custom-call(f32[8,128]{1,0:T(8,128)S(1)} %get-tuple-element.12.refs_0_, f32[32,2,128]{2,1,0:T(2,128)S(1)} %all_to_all.17.refs_1_), custom_call_target="tpu_custom_call" | custom-call | tf_op jit(solution)/shard_map/result/pallas_call | solution.py:201
  (2 shorter events, 0.0 us)
Async XLA Ops:
  0.6 0.7 %copy-start = (f32[16,64]{1,0:T(8,128)S(1)}, f32[16,64]{1,0:T(8,128)}, u32[]{:S(2)}) copy-start(f32[16,64]{1,0:T(8,128)} %panel_ref.1) | copy-start | bytes 12292
  17.5 11.3 %collective-permute-start.1 = (f32[16,8,128]{2,1,0:T(8,128)S(1)}, f32[16,8,128]{2,1,0:T(8,128)S(1)}, u32[]{:S(2)}, u32[]{:S(2)}) collective-permute-start(f32[16,8,128]{2,1,0:T(8,128)S(1)} %get-tuple-element.14), channel_id=1, source_target_pairs={{4,0},{5,32},{2,224},{3,64},{6,192},{7,96},{0,160},{1,128},{12,8},... | collective-permute-start | bytes 196616 | tf_op jit(solution)/shard_map/ppermute | solution.py:159
  24.7 5.8 %collective-permute-start = (f32[16,8,128]{2,1,0:T(8,128)S(1)}, f32[16,8,128]{2,1,0:T(8,128)S(1)}, u32[]{:S(2)}, u32[]{:S(2)}) collective-permute-start(f32[16,8,128]{2,1,0:T(8,128)S(1)} %get-tuple-element.15), channel_id=1, source_target_pairs={{4,0},{5,32},{2,224},{3,64},{6,192},{7,96},{0,160},{1,128},{12,8},... | collective-permute-start | bytes 196616 | tf_op jit(solution)/shard_map/ppermute | solution.py:160

commit v4 on v3

--- a/solution.py
+++ b/solution.py
@@ -80,7 +80,7 @@
     out_ref[...] = jnp.broadcast_to(piece[None], out_ref.shape)
 
 
-def prepare_kernel(x_ref, slab_ref, kinship_ref, high_ref, low_ref, buffer, sems):
+def prepare_kernel(slab_ref, kinship_ref, high_ref, low_ref, late_ref, buffer, sems):
     rows = kinship_ref.shape[0]
     height = rows // CHUNKS
 
@@ -89,7 +89,8 @@
 
     for i in range(CHUNKS):
         copy(i).start()
-    start = x_ref[0] * (Y * C)
+    late_ref[...] = slab_ref[slab_ref.shape[0] - late_ref.shape[0] :]
+    start = lax.axis_index("x") * (Y * C)
     own = jnp.concatenate([unpacked(slab_ref[start + j], slab_ref[start + j + 1]) for j in range(0, Y * C, 2)], axis=1)
     own = jnp.concatenate(split(own), axis=0)
     for i in range(CHUNKS):
@@ -157,20 +158,20 @@
     slab = lax.all_to_all(pieces, PLANE, 0, 0, tiled=True)
     pairs = plane_to_column()
     early = lax.ppermute(slab[: peers // 2], AXES, pairs)
-    late = lax.ppermute(slab[peers // 2 :], AXES, pairs)
-    x_index = lax.axis_index("x").reshape(1)
-    high, low = pl.pallas_call(
+    high, low, late = pl.pallas_call(
         prepare_kernel,
         out_shape=(
             jax.ShapeDtypeStruct((slab_rows + 8 * TRAITS, kinship.shape[1]), jnp.bfloat16),
             jax.ShapeDtypeStruct(kinship.shape, jnp.bfloat16),
+            jax.ShapeDtypeStruct((peers // 2, 8, 128), f32),
         ),
-        in_specs=[pl.BlockSpec(memory_space=pltpu.SMEM), VMEM, pl.BlockSpec(memory_space=pltpu.HBM)],
-        out_specs=(VMEM, VMEM),
+        in_specs=[VMEM, pl.BlockSpec(memory_space=pltpu.HBM)],
+        out_specs=(VMEM, VMEM, VMEM),
         scratch_shapes=[pltpu.VMEM((CHUNKS, slab_rows // CHUNKS, kinship.shape[1]), f32), pltpu.SemaphoreType.DMA((CHUNKS,))],
         compiler_params=WHOLE,
         name="prepare",
-    )(x_index, slab, kinship)
+    )(slab, kinship)
+    late = lax.ppermute(late, AXES, pairs)
     partial, wide = pl.pallas_call(
         first_kernel,
         out_shape=(jax.ShapeDtypeStruct((TRAITS, slab_rows), f32), jax.ShapeDtypeStruct((TRAITS, 8 * TRAITS), f32)),

time: 54.9 us -> 57.7 us (1.051)
  blocking collectives: 38.5 us -> 40 us
  waiting for transfers between devices: 1.03 us -> 2.3 us
    all_to_all x1, blocking collectives: 10.3 us -> 12.1 us  [shards(): parts = lax.all_to_all(parts, COLS, 0, 0, tiled=True)]
    ppermute x1, waiting for transfers between devices: 1.03 us -> 2.3 us  [shards(): late = lax.ppermute(late, AXES, pairs)]
where the time goes in v4:
time: 57.7 us; the launch traced here: 57.4 us
  blocking collectives  40 us (69%)
  starting transfers between devices  8.23 us (14%)
  Pallas kernels  5.51 us (10%)
  waiting for transfers between devices  2.3 us (4%)
  local copies, waits for them, and re-layouts  0.7 us (1%)
  between operations  0.65 us (1%)
    all_to_all x1, blocking collectives, shards(): slab = lax.all_to_all(pieces, PLANE, 0, 0, tiled=True)  16 us
    all_to_all x1, blocking collectives, shards(): parts = lax.all_to_all(parts, COLS, 0, 0, tiled=True)  12.1 us
    all_to_all x1, blocking collectives, shards(): scores = lax.all_to_all(scores, ROWS, 0, 0, tiled=True)  11.9 us
    ppermute x1, starting transfers between devices, shards(): early = lax.ppermute(slab[:peers // 2], AXES, pairs)  7.19 us
    pallas_call x1, Pallas kernels, shards(): pl.pallas_call(prepare_kernel, out_shape=(jax.ShapeDtypeStruct((slab_rows...  3.02 us
    ppermute x1, waiting for transfers between devices, shards(): late = lax.ppermute(late, AXES, pairs)  2.3 us
  transfers between devices with their start and end apart: 2, of which 1 were waited for; matrix products, arithmetic and copies ran while one was open for 0% of the time, Pallas kernels for 7%

profile of v4, /device:TPU:1, one launch (start us, length us, event | category | flops | bytes accessed | tf_op | source)
XLA Modules:
  0.0 57.4 jit_solution(6212558402659003248)
XLA Ops:
  0.6 0.0 copy-start
  0.6 0.7 %copy-done = f32[16,64]{1,0:T(8,128)S(1)} copy-done((f32[16,64]{1,0:T(8,128)S(1)}, f32[16,64]{1,0:T(8,128)}, u32[]{:S(2)}) %copy-start) | copy-done | bytes 4120
  1.3 0.1 pack.1
  1.4 16.0 %all_to_all.15.slab_ref = f32[32,8,128]{2,1,0:T(8,128)S(1)} all-to-all(f32[32,8,128]{2,1,0:T(8,128)S(1)} %pack.1), channel_id=1, replica_groups=mesh['z'=8,'x'=4,'y'=4,'c'=2] {'x','y','c'}, dimensions={0} | all-to-all | bytes 262144 | tf_op jit(solution)/shard_map/all_to_all | solution.py:158
  17.5 7.2 %collective-permute-start.1 = (f32[16,8,128]{2,1,0:T(8,128)S(1)}, f32[16,8,128]{2,1,0:T(8,128)S(1)}, u32[]{:S(2)}, u32[]{:S(2)}) collective-permute-start(f32[16,8,128]{2,1,0:T(8,128)S(1)} %slice.4), channel_id=1, source_target_pairs={{4,0},{5,32},{2,224},{3,64},{6,192},{7,96},{0,160},{1,128},{12,8},... | collective-permute-start | bytes 196616 | tf_op jit(solution)/shard_map/ppermute | solution.py:160
  24.6 3.0 %prepare.1 = (bf16[640,2048]{1,0:T(8,128)(2,1)S(1)}, bf16[512,2048]{1,0:T(8,128)(2,1)S(1)}, f32[16,8,128]{2,1,0:T(8,128)S(1)}) custom-call(f32[32,8,128]{2,1,0:T(8,128)S(1)} %all_to_all.15.slab_ref, f32[512,2048]{1,0:T(8,128)} %kinship_ref.1), custom_call_target="tpu_custom_call" | custom-call | tf_op jit(solution)/shard_map/prepare/pallas_call | solution.py:161
  27.7 1.0 %collective-permute-start = (f32[16,8,128]{2,1,0:T(8,128)S(1)}, f32[16,8,128]{2,1,0:T(8,128)S(1)}, u32[]{:S(2)}, u32[]{:S(2)}) collective-permute-start(f32[16,8,128]{2,1,0:T(8,128)S(1)} %get-tuple-element.9), channel_id=1, source_target_pairs={{4,0},{5,32},{2,224},{3,64},{6,192},{7,96},{0,160},{1,128},{12,8},... | collective-permute-start | bytes 196616 | tf_op jit(solution)/shard_map/ppermute | solution.py:174
  28.7 0.0 collective-permute-done.1.block_ref
  28.7 0.8 %first.1 = (f32[16,512]{1,0:T(8,128)S(1)}, f32[16,128]{1,0:T(8,128)S(1)}) custom-call(f32[16,8,128]{2,1,0:T(8,128)S(1)} %collective-permute-done.1.block_ref, bf16[640,2048]{1,0:T(8,128)(2,1)S(1)} %get-tuple-element.10.high_ref, bf16[512,2048]{1,0:T(8,128)(2,1)S(1)} %get-tuple-element.11.low_ref), custom_call_target="tpu_custom_call" | custom-call | tf_op jit(solution)/shard_map/first/pallas_call | solution.py:175
  29.5 2.3 %collective-permute-done.block_ref = f32[16,8,128]{2,1,0:T(8,128)S(1)} collective-permute-done((f32[16,8,128]{2,1,0:T(8,128)S(1)}, f32[16,8,128]{2,1,0:T(8,128)S(1)}, u32[]{:S(2)}, u32[]{:S(2)}) %collective-permute-start) | collective-permute-done | bytes 65568 | tf_op jit(solution)/shard_map/ppermute | solution.py:174
  31.8 0.9 %second.1 = f32[8,16,128]{2,1,0:T(8,128)S(1)} custom-call(f32[16,8,128]{2,1,0:T(8,128)S(1)} %collective-permute-done.block_ref, bf16[640,2048]{1,0:T(8,128)(2,1)S(1)} %get-tuple-element.10.high_ref, bf16[512,2048]{1,0:T(8,128)(2,1)S(1)} %get-tuple-element.11.low_ref, f32[16,512]{1,0:T(8,128)S(1)} %get-tuple-element.12.partial_ref, ...), custom_call_target="tpu_custom_call" | custom-call | tf_op jit(solution)/shard_map/second/pallas_call | solution.py:183
  32.6 12.1 %all_to_all.16.parts_ref = f32[8,16,128]{2,1,0:T(8,128)S(1)} all-to-all(f32[8,16,128]{2,1,0:T(8,128)S(1)} %second.1), channel_id=1, replica_groups=mesh['z'=8,'x'=4,'y'=4,'c'=2] {'y','c'}, dimensions={0} | all-to-all | bytes 131072 | tf_op jit(solution)/shard_map/all_to_all | solution.py:191
  44.8 11.9 %all_to_all.17.refs_1_ = f32[32,2,128]{2,1,0:T(2,128)S(1)} all-to-all(f32[32,2,128]{2,1,0:T(2,128)S(1)} %get-tuple-element.15), channel_id=1, replica_groups=mesh['z'=8,'x'=4,'y'=4,'c'=2] {'z','x'}, dimensions={0} | all-to-all | bytes 65536 | tf_op jit(solution)/shard_map/all_to_all | solution.py:200
  56.7 0.8 %result.1 = (f32[16,64]{1,0:T(8,128)}, f32[16,16]{1,0:T(8,128)}) custom-call(f32[8,128]{1,0:T(8,128)S(1)} %get-tuple-element.14.refs_0_, f32[32,2,128]{2,1,0:T(2,128)S(1)} %all_to_all.17.refs_1_), custom_call_target="tpu_custom_call" | custom-call | tf_op jit(solution)/shard_map/result/pallas_call | solution.py:202
  (2 shorter events, 0.0 us)
Async XLA Ops:
  0.6 0.7 %copy-start = (f32[16,64]{1,0:T(8,128)S(1)}, f32[16,64]{1,0:T(8,128)}, u32[]{:S(2)}) copy-start(f32[16,64]{1,0:T(8,128)} %panel_ref.1) | copy-start | bytes 12292
  17.5 11.3 %collective-permute-start.1 = (f32[16,8,128]{2,1,0:T(8,128)S(1)}, f32[16,8,128]{2,1,0:T(8,128)S(1)}, u32[]{:S(2)}, u32[]{:S(2)}) collective-permute-start(f32[16,8,128]{2,1,0:T(8,128)S(1)} %slice.4), channel_id=1, source_target_pairs={{4,0},{5,32},{2,224},{3,64},{6,192},{7,96},{0,160},{1,128},{12,8},... | collective-permute-start | bytes 196616 | tf_op jit(solution)/shard_map/ppermute | solution.py:160
  27.7 4.1 %collective-permute-start = (f32[16,8,128]{2,1,0:T(8,128)S(1)}, f32[16,8,128]{2,1,0:T(8,128)S(1)}, u32[]{:S(2)}, u32[]{:S(2)}) collective-permute-start(f32[16,8,128]{2,1,0:T(8,128)S(1)} %get-tuple-element.9), channel_id=1, source_target_pairs={{4,0},{5,32},{2,224},{3,64},{6,192},{7,96},{0,160},{1,128},{12,8},... | collective-permute-start | bytes 196616 | tf_op jit(solution)/shard_map/ppermute | solution.py:174

commit v5 on v2

--- a/solution.py
+++ b/solution.py
@@ -80,7 +80,7 @@
     out_ref[...] = jnp.broadcast_to(piece[None], out_ref.shape)
 
 
-def prepare_kernel(x_ref, slab_ref, kinship_ref, high_ref, low_ref, buffer, sems):
+def prepare_kernel(slab_ref, kinship_ref, high_ref, low_ref, form_ref, buffer, sems):
     rows = kinship_ref.shape[0]
     height = rows // CHUNKS
 
@@ -89,7 +89,7 @@
 
     for i in range(CHUNKS):
         copy(i).start()
-    start = x_ref[0] * (Y * C)
+    start = lax.axis_index("x") * (Y * C)
     own = jnp.concatenate([unpacked(slab_ref[start + j], slab_ref[start + j + 1]) for j in range(0, Y * C, 2)], axis=1)
     own = jnp.concatenate(split(own), axis=0)
     for i in range(CHUNKS):
@@ -97,46 +97,50 @@
         high, low = split(buffer[i])
         high_ref[pl.ds(i * height, height), :] = high
         low_ref[pl.ds(i * height, height), :] = low
-    form = nn(own, high_ref[:rows, :]) + nn(own, low_ref[:rows, :])
+    form = nn(own, high_ref[...]) + nn(own, low_ref[...])
     high, low = split(form[:TRAITS] + form[TRAITS:])
-    high_ref[rows:, :] = jnp.concatenate([high] * 4 + [low] * 4, axis=0)
-
-
-def product_kernel(block_ref, high_ref, low_ref, out_ref):
-    columns = high_ref.shape[1]
-    tiles = [unpacked(block_ref[j], block_ref[j + 1]) for j in range(0, columns // OWN, 2)]
-    panel = jnp.concatenate(split(jnp.concatenate(tiles, axis=1)), axis=0)
-    rows = low_ref.shape[0]
-    first = nt(panel, high_ref[...])
-    total = first[:, :rows] + nt(panel, low_ref[...])
-    total = total[:TRAITS] + total[TRAITS:]
-    wide = first[:TRAITS, rows:] + first[TRAITS:, rows:]
+    form_ref[...] = jnp.concatenate([high] * 4 + [low] * 4, axis=0)
+
+
+def panel_parts(early_ref, late_ref):
+    refs = [ref.at[j : j + 2] for ref in (early_ref, late_ref) for j in range(0, ref.shape[0], 2)]
+    return jnp.concatenate(split(jnp.concatenate([unpacked(ref[0], ref[1]) for ref in refs], axis=1)), axis=0)
+
+
+def score_kernel(early_ref, late_ref, form_ref, out_ref):
+    wide = nt(panel_parts(early_ref, late_ref), form_ref[...])
+    wide = wide[:TRAITS] + wide[TRAITS:]
     wide = wide + pltpu.roll(wide, HALF, 1)
     row = lax.broadcasted_iota(jnp.int32, wide.shape, 0) % 8
     lane = lax.broadcasted_iota(jnp.int32, wide.shape, 1) // TRAITS
     wide = jnp.where(row == lane, wide, 0.0)
     top = jnp.sum(wide[:8], axis=0, keepdims=True)
     bottom = jnp.sum(wide[8:], axis=0, keepdims=True)
-    score = jnp.concatenate([top, bottom, jnp.zeros((6, 128), jnp.float32)], axis=0)
+    out_ref[...] = jnp.broadcast_to(jnp.concatenate([top, bottom], axis=0)[None], out_ref.shape)
+
+
+def product_kernel(early_ref, late_ref, high_ref, low_ref, out_ref):
+    panel = panel_parts(early_ref, late_ref)
+    total = nt(panel, high_ref[...]) + nt(panel, low_ref[...])
+    total = total[:TRAITS] + total[TRAITS:]
     for y in range(Y):
         pair = packed(total[:, y * 128 : (y + 1) * 128])
         for c in range(C):
-            out_ref[y * C + c, :8, :] = pair[c]
-            out_ref[y * C + c, 8:, :] = score
-
-
-def own_kernel(parts_ref, own_ref, score_ref):
+            out_ref[y * C + c] = pair[c]
+
+
+def join_kernel(parts_ref, scores_ref, out_ref):
+    out_ref[:, :8, :] = parts_ref[...]
+    score = jnp.concatenate([jnp.sum(scores_ref[...], axis=0), jnp.zeros((6, 128), jnp.float32)], axis=0)
+    out_ref[:, 8:, :] = jnp.broadcast_to(score[None], (out_ref.shape[0], 8, 128))
+
+
+def result_kernel(parts_ref, kin_ref, score_ref, *, scale):
     total = jnp.sum(parts_ref[...], axis=0)
-    own_ref[...] = total[:8]
-    score_ref[...] = jnp.broadcast_to(total[8:10][None], score_ref.shape)
-
-
-def result_kernel(own_ref, parts_ref, kin_ref, score_ref, *, scale):
-    own = own_ref[...]
+    own = total[:8]
     kin_ref[:8, :] = own[:, :HALF]
     kin_ref[8:, :] = pltpu.roll(own, HALF, 1)[:, :HALF]
-    total = jnp.sum(parts_ref[...], axis=0)
-    rows = [total[b // 8 : b // 8 + 1, b % 8 * TRAITS : (b % 8 + 1) * TRAITS] for b in range(TRAITS)]
+    rows = [total[8 + b // 8 : 9 + b // 8, b % 8 * TRAITS : (b % 8 + 1) * TRAITS] for b in range(TRAITS)]
     score_ref[...] = jnp.concatenate(rows, axis=0).T * scale
 
 
@@ -146,47 +150,55 @@
     peers = X * Y * C
     pieces = pl.pallas_call(pack_kernel, out_shape=jax.ShapeDtypeStruct((peers, 8, 128), f32), in_specs=[VMEM], out_specs=VMEM, compiler_params=SMALL, name="pack")(panel_t)
     slab = lax.all_to_all(pieces, PLANE, 0, 0, tiled=True)
-    block = lax.ppermute(slab, AXES, plane_to_column())
-    x_index = lax.axis_index("x").reshape(1)
-    high, low = pl.pallas_call(
+    pairs = plane_to_column()
+    early = lax.ppermute(slab[: peers // 2], AXES, pairs)
+    late = lax.ppermute(slab[peers // 2 :], AXES, pairs)
+    wide = jax.ShapeDtypeStruct((8 * TRAITS, kinship.shape[1]), jnp.bfloat16)
+    half = jax.ShapeDtypeStruct(kinship.shape, jnp.bfloat16)
+    high, low, form = pl.pallas_call(
         prepare_kernel,
-        out_shape=(
-            jax.ShapeDtypeStruct((slab_rows + 8 * TRAITS, kinship.shape[1]), jnp.bfloat16),
-            jax.ShapeDtypeStruct(kinship.shape, jnp.bfloat16),
-        ),
-        in_specs=[pl.BlockSpec(memory_space=pltpu.SMEM), VMEM, pl.BlockSpec(memory_space=pltpu.HBM)],
-        out_specs=(VMEM, VMEM),
+        out_shape=(half, half, wide),
+        in_specs=[VMEM, pl.BlockSpec(memory_space=pltpu.HBM)],
+        out_specs=(VMEM, VMEM, VMEM),
         scratch_shapes=[pltpu.VMEM((CHUNKS, slab_rows // CHUNKS, kinship.shape[1]), f32), pltpu.SemaphoreType.DMA((CHUNKS,))],
         compiler_params=WHOLE,
         name="prepare",
-    )(x_index, slab, kinship)
+    )(slab, kinship)
+    scores = pl.pallas_call(
+        score_kernel,
+        out_shape=jax.ShapeDtypeStruct((Z * X, 2, 128), f32),
+        in_specs=[VMEM] * 3,
+        out_specs=VMEM,
+        compiler_params=LARGE,
+        name="score",
+    )(early, late, form)
+    scores = lax.all_to_all(scores, ROWS, 0, 0, tiled=True)
     parts = pl.pallas_call(
         product_kernel,
-        out_shape=jax.ShapeDtypeStruct((Y * C, 16, 128), f32),
-        in_specs=[VMEM, VMEM, VMEM],
+        out_shape=jax.ShapeDtypeStruct((Y * C, 8, 128), f32),
+        in_specs=[VMEM] * 4,
         out_specs=VMEM,
         compiler_params=LARGE,
         name="product",
-    )(block, high, low)
+    )(early, late, high, low)
+    parts = pl.pallas_call(
+        join_kernel,
+        out_shape=jax.ShapeDtypeStruct((Y * C, 16, 128), f32),
+        in_specs=[VMEM] * 2,
+        out_specs=VMEM,
+        compiler_params=SMALL,
+        name="join",
+    )(parts, scores)
     parts = lax.all_to_all(parts, COLS, 0, 0, tiled=True)
-    own, scores = pl.pallas_call(
-        own_kernel,
-        out_shape=(jax.ShapeDtypeStruct((8, 128), f32), jax.ShapeDtypeStruct((Z * X, 2, 128), f32)),
-        in_specs=[VMEM],
-        out_specs=(VMEM, VMEM),
-        compiler_params=SMALL,
-        name="own",
-    )(parts)
-    scores = lax.all_to_all(scores, ROWS, 0, 0, tiled=True)
     samples = OWN * Z * X * Y * C
     return pl.pallas_call(
         lambda *refs: result_kernel(*refs, scale=samples**-0.5),
         out_shape=(jax.ShapeDtypeStruct(panel_t.shape, f32), jax.ShapeDtypeStruct((TRAITS, TRAITS), f32)),
-        in_specs=[VMEM, VMEM],
+        in_specs=[VMEM],
         out_specs=(VMEM, VMEM),
         compiler_params=SMALL,
         name="result",
-    )(own, scores)
+    )(parts)
 
 
 def solution(mesh):

time: 55.3 us -> 56.7 us (1.025)
  blocking collectives: 41 us -> 23.7 us
  starting transfers between devices: 7.19 us -> 15.7 us
  waiting for transfers between devices: 0.18 us -> 6.46 us
  local copies, waits for them, and re-layouts: 0.69 us -> 3.62 us
  Pallas kernels: 5.38 us -> 6.28 us
    all_to_all x1 -> x0, blocking collectives: 16.1 us -> none  [shards(): scores = lax.all_to_all(scores, ROWS, 0, 0, tiled=True)]
    all_to_all x0 -> x1, starting transfers between devices: none -> 7.45 us  [shards(): scores = lax.all_to_all(scores, ROWS, 0, 0, tiled=True)]
    all_to_all x0 -> x1, waiting for transfers between devices: none -> 5.99 us  [shards(): scores = lax.all_to_all(scores, ROWS, 0, 0, tiled=True)]
    unnamed x2 -> x6, local copies, waits for them, and re-layouts: 0.69 us -> 3.61 us
    all_to_all x1, blocking collectives: 8.86 us -> 7.61 us  [shards(): parts = lax.all_to_all(parts, COLS, 0, 0, tiled=True)]
    ppermute x1 -> x2, starting transfers between devices: 7.19 us -> 8.23 us  [the longest x1 7.28 us: shards(): late = lax.ppermute(slab[peers // 2:], AXES, pairs)]
    pallas_call x3 -> x4, Pallas kernels: 4.52 us -> 5.45 us  [the longest x1 3.02 us: shards(): pl.pallas_call(prepare_kernel, out_shape=(half, half, wide), in_specs=[VM...]
  transfers between devices with their start and end apart: 1 -> 3, of which waited for: 1 -> 2; matrix products, arithmetic and copies ran while one was open for 0% -> 0% of each run, Pallas kernels for 6% -> 8%
where the time goes in v5:
time: 56.7 us; the launch traced here: 56.4 us
  blocking collectives  23.7 us (42%)
  starting transfers between devices  15.7 us (28%)
  waiting for transfers between devices  6.46 us (11%)
  Pallas kernels  6.28 us (11%)
  local copies, waits for them, and re-layouts  3.62 us (6%)
  between operations  0.68 us (1%)
    all_to_all x1, blocking collectives, shards(): slab = lax.all_to_all(pieces, PLANE, 0, 0, tiled=True)  16 us
    all_to_all x1, blocking collectives, shards(): parts = lax.all_to_all(parts, COLS, 0, 0, tiled=True)  7.61 us
    all_to_all x1, starting transfers between devices, shards(): scores = lax.all_to_all(scores, ROWS, 0, 0, tiled=True)  7.45 us
    ppermute x1, starting transfers between devices, shards(): late = lax.ppermute(slab[peers // 2:], AXES, pairs)  7.28 us
    all_to_all x1, waiting for transfers between devices, shards(): scores = lax.all_to_all(scores, ROWS, 0, 0, tiled=True)  5.99 us
    unnamed x6, local copies, waits for them, and re-layouts  3.61 us
    pallas_call x1, Pallas kernels, shards(): pl.pallas_call(prepare_kernel, out_shape=(half, half, wide), in_specs=[VM...  3.02 us
    pallas_call x1, Pallas kernels, shards(): pl.pallas_call(product_kernel, out_shape=jax.ShapeDtypeStruct((Y * C, 8,...  1.37 us
  transfers between devices with their start and end apart: 3, of which 2 were waited for; matrix products, arithmetic and copies ran while one was open for 0% of the time, Pallas kernels for 8%

profile of v5, /device:TPU:1, one launch (start us, length us, event | category | flops | bytes accessed | tf_op | source)
XLA Modules:
  0.0 56.4 jit_solution(9114668841641669638)
XLA Ops:
  0.6 0.0 copy-start.2
  0.6 0.7 %copy-done.2 = f32[16,64]{1,0:T(8,128)S(1)} copy-done((f32[16,64]{1,0:T(8,128)S(1)}, f32[16,64]{1,0:T(8,128)}, u32[]{:S(2)}) %copy-start.2) | copy-done | bytes 4120
  1.3 0.1 pack.1
  1.4 16.0 %all_to_all.15.slab_ref = f32[32,8,128]{2,1,0:T(8,128)S(1)} all-to-all(f32[32,8,128]{2,1,0:T(8,128)S(1)} %pack.1), channel_id=1, replica_groups=mesh['z'=8,'x'=4,'y'=4,'c'=2] {'x','y','c'}, dimensions={0} | all-to-all | bytes 262144 | tf_op jit(solution)/shard_map/all_to_all | solution.py:152
  17.5 7.3 %collective-permute-start.1 = (f32[16,8,128]{2,1,0:T(8,128)S(1)}, f32[16,8,128]{2,1,0:T(8,128)S(1)}, u32[]{:S(2)}, u32[]{:S(2)}) collective-permute-start(f32[16,8,128]{2,1,0:T(8,128)S(1)} %get-tuple-element.8), channel_id=1, source_target_pairs={{4,0},{5,32},{2,224},{3,64},{6,192},{7,96},{0,160},{1,128},{12,8},... | collective-permute-start | bytes 196616 | tf_op jit(solution)/shard_map/ppermute | solution.py:155
  24.7 1.0 %collective-permute-start = (f32[16,8,128]{2,1,0:T(8,128)S(1)}, f32[16,8,128]{2,1,0:T(8,128)S(1)}, u32[]{:S(2)}, u32[]{:S(2)}) collective-permute-start(f32[16,8,128]{2,1,0:T(8,128)S(1)} %get-tuple-element.9), channel_id=1, source_target_pairs={{4,0},{5,32},{2,224},{3,64},{6,192},{7,96},{0,160},{1,128},{12,8},... | collective-permute-start | bytes 196616 | tf_op jit(solution)/shard_map/ppermute | solution.py:154
  25.7 3.0 %prepare.1 = (bf16[512,2048]{1,0:T(8,128)(2,1)S(1)}, bf16[512,2048]{1,0:T(8,128)(2,1)S(1)}, bf16[128,2048]{1,0:T(8,128)(2,1)S(1)}) custom-call(f32[32,8,128]{2,1,0:T(8,128)S(1)} %all_to_all.15.slab_ref, f32[512,2048]{1,0:T(8,128)} %kinship_ref.1), custom_call_target="tpu_custom_call" | custom-call | tf_op jit(solution)/shard_map/prepare/pallas_call | solution.py:158
  28.7 0.0 copy-start
  28.7 1.3 %copy-done = bf16[512,2048]{1,0:T(8,128)(2,1)} copy-done((bf16[512,2048]{1,0:T(8,128)(2,1)}, bf16[512,2048]{1,0:T(8,128)(2,1)S(1)}, u32[]{:S(2)}) %copy-start) | copy-done | bytes 2097176
  30.1 0.0 collective-permute-done.1.late_ref
  30.1 0.5 collective-permute-done.early_ref
  30.5 1.0 %score.1 = f32[32,2,128]{2,1,0:T(2,128)} custom-call(f32[16,8,128]{2,1,0:T(8,128)S(1)} %collective-permute-done.early_ref, f32[16,8,128]{2,1,0:T(8,128)S(1)} %collective-permute-done.1.late_ref, bf16[128,2048]{1,0:T(8,128)(2,1)S(1)} %get-tuple-element.7.form_ref), custom_call_target="tpu_custom_call" | custom-call | tf_op jit(solution)/shard_map/score/pallas_call | solution.py:167
  31.6 7.4 %all-to-all-start.1 = ((f32[32,2,128]{2,1,0:T(2,128)}), f32[32,2,128]{2,1,0:T(2,128)S(1)}, u32[]{:S(2)}, u32[]{:S(2)}) async-start(f32[32,2,128]{2,1,0:T(2,128)} %score.1), calls=%async_computation.1 | async-start | bytes 65536 | tf_op jit(solution)/shard_map/all_to_all | solution.py:175
  39.0 0.0 copy-start.1
  39.0 1.6 %copy-done.1 = bf16[512,2048]{1,0:T(8,128)(2,1)S(1)} copy-done((bf16[512,2048]{1,0:T(8,128)(2,1)S(1)}, bf16[512,2048]{1,0:T(8,128)(2,1)}, u32[]{:S(2)}) %copy-start.1) | copy-done | bytes 2097176
  40.6 1.4 %product.1.parts_ref = f32[8,8,128]{2,1,0:T(8,128)S(1)} custom-call(f32[16,8,128]{2,1,0:T(8,128)S(1)} %collective-permute-done.early_ref, f32[16,8,128]{2,1,0:T(8,128)S(1)} %collective-permute-done.1.late_ref, bf16[512,2048]{1,0:T(8,128)(2,1)S(1)} %get-tuple-element.5.high_ref, bf16[512,2048]{1,0:T(8,128)(2,1)S(1)} %copy-done.1), custom_call_target="tpu_custom_call" | custom-call | tf_op jit(solution)/shard_map/product/pallas_call | solution.py:176
  42.0 6.0 %all-to-all-done.1.scores_ref = f32[32,2,128]{2,1,0:T(2,128)S(1)} async-done(((f32[32,2,128]{2,1,0:T(2,128)}), f32[32,2,128]{2,1,0:T(2,128)S(1)}, u32[]{:S(2)}, u32[]{:S(2)}) %all-to-all-start.1) | async-done | bytes 32800 | tf_op jit(solution)/shard_map/all_to_all | solution.py:175
  48.0 7.6 %all_to_all.16.refs_0_ = f32[8,16,128]{2,1,0:T(8,128)S(1)} all-to-all(f32[8,16,128]{2,1,0:T(8,128)S(1)} %join.1), channel_id=1, replica_groups=mesh['z'=8,'x'=4,'y'=4,'c'=2] {'y','c'}, dimensions={0} | all-to-all | bytes 131072 | tf_op jit(solution)/shard_map/all_to_all | solution.py:192
  55.6 0.8 %result.1 = (f32[16,64]{1,0:T(8,128)}, f32[16,16]{1,0:T(8,128)}) custom-call(f32[8,16,128]{2,1,0:T(8,128)S(1)} %all_to_all.16.refs_0_), custom_call_target="tpu_custom_call" | custom-call | tf_op jit(solution)/shard_map/result/pallas_call | solution.py:194
  (2 shorter events, 0.0 us)
Async XLA Ops:
  0.6 0.7 %copy-start.2 = (f32[16,64]{1,0:T(8,128)S(1)}, f32[16,64]{1,0:T(8,128)}, u32[]{:S(2)}) copy-start(f32[16,64]{1,0:T(8,128)} %panel_ref.1) | copy-start | bytes 12292
  17.5 12.6 %collective-permute-start.1 = (f32[16,8,128]{2,1,0:T(8,128)S(1)}, f32[16,8,128]{2,1,0:T(8,128)S(1)}, u32[]{:S(2)}, u32[]{:S(2)}) collective-permute-start(f32[16,8,128]{2,1,0:T(8,128)S(1)} %get-tuple-element.8), channel_id=1, source_target_pairs={{4,0},{5,32},{2,224},{3,64},{6,192},{7,96},{0,160},{1,128},{12,8},... | collective-permute-start | bytes 196616 | tf_op jit(solution)/shard_map/ppermute | solution.py:155
  24.7 5.8 %collective-permute-start = (f32[16,8,128]{2,1,0:T(8,128)S(1)}, f32[16,8,128]{2,1,0:T(8,128)S(1)}, u32[]{:S(2)}, u32[]{:S(2)}) collective-permute-start(f32[16,8,128]{2,1,0:T(8,128)S(1)} %get-tuple-element.9), channel_id=1, source_target_pairs={{4,0},{5,32},{2,224},{3,64},{6,192},{7,96},{0,160},{1,128},{12,8},... | collective-permute-start | bytes 196616 | tf_op jit(solution)/shard_map/ppermute | solution.py:154
  28.7 1.3 %copy-start = (bf16[512,2048]{1,0:T(8,128)(2,1)}, bf16[512,2048]{1,0:T(8,128)(2,1)S(1)}, u32[]{:S(2)}) copy-start(bf16[512,2048]{1,0:T(8,128)(2,1)S(1)} %get-tuple-element.6.low_ref) | copy-start | bytes 6291460
  31.6 16.4 %all-to-all-start.1 = ((f32[32,2,128]{2,1,0:T(2,128)}), f32[32,2,128]{2,1,0:T(2,128)S(1)}, u32[]{:S(2)}, u32[]{:S(2)}) async-start(f32[32,2,128]{2,1,0:T(2,128)} %score.1), calls=%async_computation.1 | async-start | bytes 65536 | tf_op jit(solution)/shard_map/all_to_all | solution.py:175
  39.0 1.6 %copy-start.1 = (bf16[512,2048]{1,0:T(8,128)(2,1)S(1)}, bf16[512,2048]{1,0:T(8,128)(2,1)}, u32[]{:S(2)}) copy-start(bf16[512,2048]{1,0:T(8,128)(2,1)} %copy-done) | copy-start | bytes 6291460

commit v6 on v3

--- a/solution.py
+++ b/solution.py
@@ -1,5 +1,3 @@
-import itertools
-
 import jax
 import jax.numpy as jnp
 from jax import lax
@@ -27,21 +25,22 @@
     return ((z * X + x) * Y + y) * C + c
 
 
-def apart(a, b, n):
-    d = abs(a - b) % n
-    return min(d, n - d)
+SENDER = (
+    (7, 1, 5, 3, 0, 2, 6, 4),
+    (4, 2, 5, 3, 6, 1, 0, 7),
+    (6, 7, 0, 1, 5, 3, 4, 2),
+    (0, 5, 7, 4, 6, 1, 2, 3),
+    (0, 4, 2, 1, 3, 7, 6, 5),
+    (1, 7, 5, 3, 4, 0, 2, 6),
+    (7, 2, 4, 1, 3, 6, 0, 5),
+    (2, 4, 1, 6, 7, 5, 3, 0),
+)
 
 
 def plane_to_column():
-    pairs = []
-    for plane in range(Z):
-        y_to, c_to = divmod(plane, C)
-        senders = sorted(itertools.product(range(Y), range(C)), key=lambda s: (-apart(s[0], y_to, Y), (s[0] - y_to) % Y, s[1] != c_to))
-        planes = sorted(range(Z), key=lambda z: (apart(z, plane, Z), (z - plane) % Z))
-        for x in range(X):
-            for (y, c), z in zip(senders, planes):
-                pairs.append((number(plane, x, y, c), number(z, x, y_to, c_to)))
-    return pairs
+    return [
+        (number(p, x, *divmod(SENDER[p][z], C)), number(z, x, *divmod(p, C))) for p in range(Z) for x in range(X) for z in range(Z)
+    ]
 
 
 def low_lanes(shape):
@@ -80,7 +79,7 @@
     out_ref[...] = jnp.broadcast_to(piece[None], out_ref.shape)
 
 
-def prepare_kernel(x_ref, slab_ref, kinship_ref, high_ref, low_ref, buffer, sems):
+def prepare_kernel(slab_ref, kinship_ref, high_ref, low_ref, buffer, sems):
     rows = kinship_ref.shape[0]
     height = rows // CHUNKS
 
@@ -89,7 +88,7 @@
 
     for i in range(CHUNKS):
         copy(i).start()
-    start = x_ref[0] * (Y * C)
+    start = lax.axis_index("x") * (Y * C)
     own = jnp.concatenate([unpacked(slab_ref[start + j], slab_ref[start + j + 1]) for j in range(0, Y * C, 2)], axis=1)
     own = jnp.concatenate(split(own), axis=0)
     for i in range(CHUNKS):
@@ -158,19 +157,18 @@
     pairs = plane_to_column()
     early = lax.ppermute(slab[: peers // 2], AXES, pairs)
     late = lax.ppermute(slab[peers // 2 :], AXES, pairs)
-    x_index = lax.axis_index("x").reshape(1)
     high, low = pl.pallas_call(
         prepare_kernel,
         out_shape=(
             jax.ShapeDtypeStruct((slab_rows + 8 * TRAITS, kinship.shape[1]), jnp.bfloat16),
             jax.ShapeDtypeStruct(kinship.shape, jnp.bfloat16),
         ),
-        in_specs=[pl.BlockSpec(memory_space=pltpu.SMEM), VMEM, pl.BlockSpec(memory_space=pltpu.HBM)],
+        in_specs=[VMEM, pl.BlockSpec(memory_space=pltpu.HBM)],
         out_specs=(VMEM, VMEM),
         scratch_shapes=[pltpu.VMEM((CHUNKS, slab_rows // CHUNKS, kinship.shape[1]), f32), pltpu.SemaphoreType.DMA((CHUNKS,))],
         compiler_params=WHOLE,
         name="prepare",
-    )(x_index, slab, kinship)
+    )(slab, kinship)
     partial, wide = pl.pallas_call(
         first_kernel,
         out_shape=(jax.ShapeDtypeStruct((TRAITS, slab_rows), f32), jax.ShapeDtypeStruct((TRAITS, 8 * TRAITS), f32)),

time: 54.9 us -> 56.8 us (1.035)
  blocking collectives: 38.5 us -> 42.1 us
  waiting for transfers between devices: 1.03 us -> 0.01 us
  starting transfers between devices: 8.23 us -> 7.56 us
    ppermute x1, starting transfers between devices: 7.28 us -> 2 us  [shards(): early = lax.ppermute(slab[:peers // 2], AXES, pairs)]
    ppermute x1, starting transfers between devices: 0.96 us -> 5.56 us  [shards(): late = lax.ppermute(slab[peers // 2:], AXES, pairs)]
    all_to_all x1, blocking collectives: 10.3 us -> 14.4 us  [shards(): parts = lax.all_to_all(parts, COLS, 0, 0, tiled=True)]
    ppermute x1, waiting for transfers between devices: 1.03 us -> 0.01 us  [shards(): late = lax.ppermute(slab[peers // 2:], AXES, pairs)]
  transfers between devices with their start and end apart: 2 -> 2, of which waited for: 1 -> 0; matrix products, arithmetic and copies ran while one was open for 0% -> 0% of each run, Pallas kernels for 7% -> 7%
where the time goes in v6:
time: 56.8 us; the launch traced here: 56.5 us
  blocking collectives  42.1 us (74%)
  starting transfers between devices  7.56 us (13%)
  Pallas kernels  5.52 us (10%)
  local copies, waits for them, and re-layouts  0.7 us (1%)
  between operations  0.68 us (1%)
    all_to_all x1, blocking collectives, shards(): slab = lax.all_to_all(pieces, PLANE, 0, 0, tiled=True)  16 us
    all_to_all x1, blocking collectives, shards(): parts = lax.all_to_all(parts, COLS, 0, 0, tiled=True)  14.4 us
    all_to_all x1, blocking collectives, shards(): scores = lax.all_to_all(scores, ROWS, 0, 0, tiled=True)  11.6 us
    ppermute x1, starting transfers between devices, shards(): late = lax.ppermute(slab[peers // 2:], AXES, pairs)  5.56 us
    pallas_call x1, Pallas kernels, shards(): pl.pallas_call(prepare_kernel, out_shape=(jax.ShapeDtypeStruct((slab_rows...  3.02 us
    ppermute x1, starting transfers between devices, shards(): early = lax.ppermute(slab[:peers // 2], AXES, pairs)  2 us
  transfers between devices with their start and end apart: 2, of which 0 were waited for; matrix products, arithmetic and copies ran while one was open for 0% of the time, Pallas kernels for 7%

profile of v6, /device:TPU:1, one launch (start us, length us, event | category | flops | bytes accessed | tf_op | source)
XLA Modules:
  0.0 56.5 jit_solution(13159740264531287963)
XLA Ops:
  0.6 0.0 copy-start
  0.6 0.7 %copy-done = f32[16,64]{1,0:T(8,128)S(1)} copy-done((f32[16,64]{1,0:T(8,128)S(1)}, f32[16,64]{1,0:T(8,128)}, u32[]{:S(2)}) %copy-start) | copy-done | bytes 4120
  1.3 0.1 pack.1
  1.4 16.0 %all_to_all.15.slab_ref = f32[32,8,128]{2,1,0:T(8,128)S(1)} all-to-all(f32[32,8,128]{2,1,0:T(8,128)S(1)} %pack.1), channel_id=1, replica_groups=mesh['z'=8,'x'=4,'y'=4,'c'=2] {'x','y','c'}, dimensions={0} | all-to-all | bytes 262144 | tf_op jit(solution)/shard_map/all_to_all | solution.py:156
  17.5 2.0 %collective-permute-start.1 = (f32[16,8,128]{2,1,0:T(8,128)S(1)}, f32[16,8,128]{2,1,0:T(8,128)S(1)}, u32[]{:S(2)}, u32[]{:S(2)}) collective-permute-start(f32[16,8,128]{2,1,0:T(8,128)S(1)} %get-tuple-element.14), channel_id=1, source_target_pairs={{7,0},{1,32},{5,64},{3,96},{0,128},{2,160},{6,192},{4,224},{15,8},... | collective-permute-start | bytes 196616 | tf_op jit(solution)/shard_map/ppermute | solution.py:158
  19.5 5.6 %collective-permute-start = (f32[16,8,128]{2,1,0:T(8,128)S(1)}, f32[16,8,128]{2,1,0:T(8,128)S(1)}, u32[]{:S(2)}, u32[]{:S(2)}) collective-permute-start(f32[16,8,128]{2,1,0:T(8,128)S(1)} %get-tuple-element.15), channel_id=1, source_target_pairs={{7,0},{1,32},{5,64},{3,96},{0,128},{2,160},{6,192},{4,224},{15,8},... | collective-permute-start | bytes 196616 | tf_op jit(solution)/shard_map/ppermute | solution.py:159
  25.0 3.0 %prepare.1 = (bf16[640,2048]{1,0:T(8,128)(2,1)S(1)}, bf16[512,2048]{1,0:T(8,128)(2,1)S(1)}) custom-call(f32[32,8,128]{2,1,0:T(8,128)S(1)} %all_to_all.15.slab_ref, f32[512,2048]{1,0:T(8,128)} %kinship_ref.1), custom_call_target="tpu_custom_call" | custom-call | tf_op jit(solution)/shard_map/prepare/pallas_call | solution.py:160
  28.1 0.0 collective-permute-done.1.block_ref
  28.1 0.8 %first.1 = (f32[16,512]{1,0:T(8,128)S(1)}, f32[16,128]{1,0:T(8,128)S(1)}) custom-call(f32[16,8,128]{2,1,0:T(8,128)S(1)} %collective-permute-done.1.block_ref, bf16[640,2048]{1,0:T(8,128)(2,1)S(1)} %get-tuple-element.8.high_ref, bf16[512,2048]{1,0:T(8,128)(2,1)S(1)} %get-tuple-element.9.low_ref), custom_call_target="tpu_custom_call" | custom-call | tf_op jit(solution)/shard_map/first/pallas_call | solution.py:172
  28.8 0.0 collective-permute-done.block_ref
  28.8 0.9 %second.1 = f32[8,16,128]{2,1,0:T(8,128)S(1)} custom-call(f32[16,8,128]{2,1,0:T(8,128)S(1)} %collective-permute-done.block_ref, bf16[640,2048]{1,0:T(8,128)(2,1)S(1)} %get-tuple-element.8.high_ref, bf16[512,2048]{1,0:T(8,128)(2,1)S(1)} %get-tuple-element.9.low_ref, f32[16,512]{1,0:T(8,128)S(1)} %get-tuple-element.10.partial_ref, ...), custom_call_target="tpu_custom_call" | custom-call | tf_op jit(solution)/shard_map/second/pallas_call | solution.py:180
  29.7 14.4 %all_to_all.16.parts_ref = f32[8,16,128]{2,1,0:T(8,128)S(1)} all-to-all(f32[8,16,128]{2,1,0:T(8,128)S(1)} %second.1), channel_id=1, replica_groups=mesh['z'=8,'x'=4,'y'=4,'c'=2] {'y','c'}, dimensions={0} | all-to-all | bytes 131072 | tf_op jit(solution)/shard_map/all_to_all | solution.py:188
  44.2 11.6 %all_to_all.17.refs_1_ = f32[32,2,128]{2,1,0:T(2,128)S(1)} all-to-all(f32[32,2,128]{2,1,0:T(2,128)S(1)} %get-tuple-element.13), channel_id=1, replica_groups=mesh['z'=8,'x'=4,'y'=4,'c'=2] {'z','x'}, dimensions={0} | all-to-all | bytes 65536 | tf_op jit(solution)/shard_map/all_to_all | solution.py:197
  55.8 0.8 %result.1 = (f32[16,64]{1,0:T(8,128)}, f32[16,16]{1,0:T(8,128)}) custom-call(f32[8,128]{1,0:T(8,128)S(1)} %get-tuple-element.12.refs_0_, f32[32,2,128]{2,1,0:T(2,128)S(1)} %all_to_all.17.refs_1_), custom_call_target="tpu_custom_call" | custom-call | tf_op jit(solution)/shard_map/result/pallas_call | solution.py:199
  (2 shorter events, 0.0 us)
Async XLA Ops:
  0.6 0.7 %copy-start = (f32[16,64]{1,0:T(8,128)S(1)}, f32[16,64]{1,0:T(8,128)}, u32[]{:S(2)}) copy-start(f32[16,64]{1,0:T(8,128)} %panel_ref.1) | copy-start | bytes 12292
  17.5 10.6 %collective-permute-start.1 = (f32[16,8,128]{2,1,0:T(8,128)S(1)}, f32[16,8,128]{2,1,0:T(8,128)S(1)}, u32[]{:S(2)}, u32[]{:S(2)}) collective-permute-start(f32[16,8,128]{2,1,0:T(8,128)S(1)} %get-tuple-element.14), channel_id=1, source_target_pairs={{7,0},{1,32},{5,64},{3,96},{0,128},{2,160},{6,192},{4,224},{15,8},... | collective-permute-start | bytes 196616 | tf_op jit(solution)/shard_map/ppermute | solution.py:158
  19.5 9.4 %collective-permute-start = (f32[16,8,128]{2,1,0:T(8,128)S(1)}, f32[16,8,128]{2,1,0:T(8,128)S(1)}, u32[]{:S(2)}, u32[]{:S(2)}) collective-permute-start(f32[16,8,128]{2,1,0:T(8,128)S(1)} %get-tuple-element.15), channel_id=1, source_target_pairs={{7,0},{1,32},{5,64},{3,96},{0,128},{2,160},{6,192},{4,224},{15,8},... | collective-permute-start | bytes 196616 | tf_op jit(solution)/shard_map/ppermute | solution.py:159

commit v7 on v2

--- a/solution.py
+++ b/solution.py
@@ -1,5 +1,3 @@
-import itertools
-
 import jax
 import jax.numpy as jnp
 from jax import lax
@@ -27,21 +25,22 @@
     return ((z * X + x) * Y + y) * C + c
 
 
-def apart(a, b, n):
-    d = abs(a - b) % n
-    return min(d, n - d)
+SENDER = (
+    (7, 1, 5, 3, 0, 2, 6, 4),
+    (4, 2, 5, 3, 6, 1, 0, 7),
+    (6, 7, 0, 1, 5, 3, 4, 2),
+    (0, 5, 7, 4, 6, 1, 2, 3),
+    (0, 4, 2, 1, 3, 7, 6, 5),
+    (1, 7, 5, 3, 4, 0, 2, 6),
+    (7, 2, 4, 1, 3, 6, 0, 5),
+    (2, 4, 1, 6, 7, 5, 3, 0),
+)
 
 
 def plane_to_column():
-    pairs = []
-    for plane in range(Z):
-        y_to, c_to = divmod(plane, C)
-        senders = sorted(itertools.product(range(Y), range(C)), key=lambda s: (-apart(s[0], y_to, Y), (s[0] - y_to) % Y, s[1] != c_to))
-        planes = sorted(range(Z), key=lambda z: (apart(z, plane, Z), (z - plane) % Z))
-        for x in range(X):
-            for (y, c), z in zip(senders, planes):
-                pairs.append((number(plane, x, y, c), number(z, x, y_to, c_to)))
-    return pairs
+    return [
+        (number(p, x, *divmod(SENDER[p][z], C)), number(z, x, *divmod(p, C))) for p in range(Z) for x in range(X) for z in range(Z)
+    ]
 
 
 def low_lanes(shape):
@@ -80,7 +79,7 @@
     out_ref[...] = jnp.broadcast_to(piece[None], out_ref.shape)
 
 
-def prepare_kernel(x_ref, slab_ref, kinship_ref, high_ref, low_ref, buffer, sems):
+def prepare_kernel(slab_ref, kinship_ref, high_ref, low_ref, buffer, sems):
     rows = kinship_ref.shape[0]
     height = rows // CHUNKS
 
@@ -89,7 +88,7 @@
 
     for i in range(CHUNKS):
         copy(i).start()
-    start = x_ref[0] * (Y * C)
+    start = lax.axis_index("x") * (Y * C)
     own = jnp.concatenate([unpacked(slab_ref[start + j], slab_ref[start + j + 1]) for j in range(0, Y * C, 2)], axis=1)
     own = jnp.concatenate(split(own), axis=0)
     for i in range(CHUNKS):
@@ -147,19 +146,18 @@
     pieces = pl.pallas_call(pack_kernel, out_shape=jax.ShapeDtypeStruct((peers, 8, 128), f32), in_specs=[VMEM], out_specs=VMEM, compiler_params=SMALL, name="pack")(panel_t)
     slab = lax.all_to_all(pieces, PLANE, 0, 0, tiled=True)
     block = lax.ppermute(slab, AXES, plane_to_column())
-    x_index = lax.axis_index("x").reshape(1)
     high, low = pl.pallas_call(
         prepare_kernel,
         out_shape=(
             jax.ShapeDtypeStruct((slab_rows + 8 * TRAITS, kinship.shape[1]), jnp.bfloat16),
             jax.ShapeDtypeStruct(kinship.shape, jnp.bfloat16),
         ),
-        in_specs=[pl.BlockSpec(memory_space=pltpu.SMEM), VMEM, pl.BlockSpec(memory_space=pltpu.HBM)],
+        in_specs=[VMEM, pl.BlockSpec(memory_space=pltpu.HBM)],
         out_specs=(VMEM, VMEM),
         scratch_shapes=[pltpu.VMEM((CHUNKS, slab_rows // CHUNKS, kinship.shape[1]), f32), pltpu.SemaphoreType.DMA((CHUNKS,))],
         compiler_params=WHOLE,
         name="prepare",
-    )(x_index, slab, kinship)
+    )(slab, kinship)
     parts = pl.pallas_call(
         product_kernel,
         out_shape=jax.ShapeDtypeStruct((Y * C, 16, 128), f32),

time: 55.3 us -> 56.6 us (1.024)
  starting transfers between devices: 7.19 us -> 1.92 us
  blocking collectives: 41 us -> 45.9 us
  waiting for transfers between devices: 0.18 us -> 1.85 us
    ppermute x1, starting transfers between devices: 7.19 us -> 1.92 us  [shards(): block = lax.ppermute(slab, AXES, plane_to_column())]
    all_to_all x1, blocking collectives: 8.86 us -> 13 us  [shards(): parts = lax.all_to_all(parts, COLS, 0, 0, tiled=True)]
    ppermute x1, waiting for transfers between devices: 0.18 us -> 1.85 us  [shards(): block = lax.ppermute(slab, AXES, plane_to_column())]
    all_to_all x1, blocking collectives: 16.1 us -> 16.8 us  [shards(): scores = lax.all_to_all(scores, ROWS, 0, 0, tiled=True)]
  transfers between devices with their start and end apart: 1 -> 1, of which waited for: 1 -> 1; matrix products, arithmetic and copies ran while one was open for 0% -> 0% of each run, Pallas kernels for 6% -> 5%
where the time goes in v7:
time: 56.6 us; the launch traced here: 56.4 us
  blocking collectives  45.9 us (81%)
  Pallas kernels  5.36 us (9%)
  starting transfers between devices  1.92 us (3%)
  waiting for transfers between devices  1.85 us (3%)
  local copies, waits for them, and re-layouts  0.69 us (1%)
  between operations  0.65 us (1%)
    all_to_all x1, blocking collectives, shards(): scores = lax.all_to_all(scores, ROWS, 0, 0, tiled=True)  16.8 us
    all_to_all x1, blocking collectives, shards(): slab = lax.all_to_all(pieces, PLANE, 0, 0, tiled=True)  16 us
    all_to_all x1, blocking collectives, shards(): parts = lax.all_to_all(parts, COLS, 0, 0, tiled=True)  13 us
    pallas_call x1, Pallas kernels, shards(): pl.pallas_call(prepare_kernel, out_shape=(jax.ShapeDtypeStruct((slab_rows...  3.02 us
    ppermute x1, starting transfers between devices, shards(): block = lax.ppermute(slab, AXES, plane_to_column())  1.92 us
    ppermute x1, waiting for transfers between devices, shards(): block = lax.ppermute(slab, AXES, plane_to_column())  1.85 us
    pallas_call x1, Pallas kernels, shards(): pl.pallas_call(product_kernel, out_shape=jax.ShapeDtypeStruct((Y * C, 16,...  1.46 us
  transfers between devices with their start and end apart: 1, of which 1 were waited for; matrix products, arithmetic and copies ran while one was open for 0% of the time, Pallas kernels for 5%

profile of v7, /device:TPU:1, one launch (start us, length us, event | category | flops | bytes accessed | tf_op | source)
XLA Modules:
  0.0 56.4 jit_solution(6979432822551375658)
XLA Ops:
  0.6 0.0 copy-start
  0.6 0.7 %copy-done = f32[16,64]{1,0:T(8,128)S(1)} copy-done((f32[16,64]{1,0:T(8,128)S(1)}, f32[16,64]{1,0:T(8,128)}, u32[]{:S(2)}) %copy-start) | copy-done | bytes 4120
  1.3 0.1 pack.1
  1.4 16.0 %all_to_all.15.slab_ref = f32[32,8,128]{2,1,0:T(8,128)S(1)} all-to-all(f32[32,8,128]{2,1,0:T(8,128)S(1)} %pack.1), channel_id=1, replica_groups=mesh['z'=8,'x'=4,'y'=4,'c'=2] {'x','y','c'}, dimensions={0} | all-to-all | bytes 262144 | tf_op jit(solution)/shard_map/all_to_all | solution.py:147
  17.5 1.9 %collective-permute-start = (f32[32,8,128]{2,1,0:T(8,128)S(1)}, f32[32,8,128]{2,1,0:T(8,128)S(1)}, u32[]{:S(2)}, u32[]{:S(2)}) collective-permute-start(f32[32,8,128]{2,1,0:T(8,128)S(1)} %all_to_all.15.slab_ref), channel_id=1, source_target_pairs={{7,0},{1,32},{5,64},{3,96},{0,128},{2,160},{6,192},{4,224},{15,8},... | collective-permute-start | bytes 393224 | tf_op jit(solution)/shard_map/ppermute | solution.py:148
  19.4 3.0 %prepare.1 = (bf16[640,2048]{1,0:T(8,128)(2,1)S(1)}, bf16[512,2048]{1,0:T(8,128)(2,1)S(1)}) custom-call(f32[32,8,128]{2,1,0:T(8,128)S(1)} %all_to_all.15.slab_ref, f32[512,2048]{1,0:T(8,128)} %kinship_ref.1), custom_call_target="tpu_custom_call" | custom-call | tf_op jit(solution)/shard_map/prepare/pallas_call | solution.py:149
  22.4 1.8 %collective-permute-done.block_ref = f32[32,8,128]{2,1,0:T(8,128)S(1)} collective-permute-done((f32[32,8,128]{2,1,0:T(8,128)S(1)}, f32[32,8,128]{2,1,0:T(8,128)S(1)}, u32[]{:S(2)}, u32[]{:S(2)}) %collective-permute-start) | collective-permute-done | bytes 131104 | tf_op jit(solution)/shard_map/ppermute | solution.py:148
  24.3 1.5 %product.1 = f32[8,16,128]{2,1,0:T(8,128)S(1)} custom-call(f32[32,8,128]{2,1,0:T(8,128)S(1)} %collective-permute-done.block_ref, bf16[640,2048]{1,0:T(8,128)(2,1)S(1)} %get-tuple-element.6.high_ref, bf16[512,2048]{1,0:T(8,128)(2,1)S(1)} %get-tuple-element.7.low_ref), custom_call_target="tpu_custom_call" | custom-call | tf_op jit(solution)/shard_map/product/pallas_call | solution.py:161
  25.7 13.0 %all_to_all.16.parts_ref = f32[8,16,128]{2,1,0:T(8,128)S(1)} all-to-all(f32[8,16,128]{2,1,0:T(8,128)S(1)} %product.1), channel_id=1, replica_groups=mesh['z'=8,'x'=4,'y'=4,'c'=2] {'y','c'}, dimensions={0} | all-to-all | bytes 131072 | tf_op jit(solution)/shard_map/all_to_all | solution.py:169
  38.7 16.8 %all_to_all.17.refs_1_ = f32[32,2,128]{2,1,0:T(2,128)S(1)} all-to-all(f32[32,2,128]{2,1,0:T(2,128)S(1)} %get-tuple-element.9), channel_id=1, replica_groups=mesh['z'=8,'x'=4,'y'=4,'c'=2] {'z','x'}, dimensions={0} | all-to-all | bytes 65536 | tf_op jit(solution)/shard_map/all_to_all | solution.py:178
  55.6 0.8 %result.1 = (f32[16,64]{1,0:T(8,128)}, f32[16,16]{1,0:T(8,128)}) custom-call(f32[8,128]{1,0:T(8,128)S(1)} %get-tuple-element.8.refs_0_, f32[32,2,128]{2,1,0:T(2,128)S(1)} %all_to_all.17.refs_1_), custom_call_target="tpu_custom_call" | custom-call | tf_op jit(solution)/shard_map/result/pallas_call | solution.py:180
  (1 shorter events, 0.0 us)
Async XLA Ops:
  0.6 0.7 %copy-start = (f32[16,64]{1,0:T(8,128)S(1)}, f32[16,64]{1,0:T(8,128)}, u32[]{:S(2)}) copy-start(f32[16,64]{1,0:T(8,128)} %panel_ref.1) | copy-start | bytes 12292
  17.5 6.8 %collective-permute-start = (f32[32,8,128]{2,1,0:T(8,128)S(1)}, f32[32,8,128]{2,1,0:T(8,128)S(1)}, u32[]{:S(2)}, u32[]{:S(2)}) collective-permute-start(f32[32,8,128]{2,1,0:T(8,128)S(1)} %all_to_all.15.slab_ref), channel_id=1, source_target_pairs={{7,0},{1,32},{5,64},{3,96},{0,128},{2,160},{6,192},{4,224},{15,8},... | collective-permute-start | bytes 393224 | tf_op jit(solution)/shard_map/ppermute | solution.py:148

commit v8 on v2

--- a/solution.py
+++ b/solution.py
@@ -15,6 +15,7 @@
 PLANE = ("x", "y", "c")
 TRAITS = 16
 OWN = 64
+PARTS = 2
 CHUNKS = 8
 HALF = 64
 VMEM = pl.BlockSpec(memory_space=pltpu.VMEM)
@@ -80,7 +81,7 @@
     out_ref[...] = jnp.broadcast_to(piece[None], out_ref.shape)
 
 
-def prepare_kernel(x_ref, slab_ref, kinship_ref, high_ref, low_ref, buffer, sems):
+def prepare_kernel(slab_ref, kinship_ref, high_ref, low_ref, buffer, sems):
     rows = kinship_ref.shape[0]
     height = rows // CHUNKS
 
@@ -89,7 +90,7 @@
 
     for i in range(CHUNKS):
         copy(i).start()
-    start = x_ref[0] * (Y * C)
+    start = lax.axis_index("x") * (Y * C)
     own = jnp.concatenate([unpacked(slab_ref[start + j], slab_ref[start + j + 1]) for j in range(0, Y * C, 2)], axis=1)
     own = jnp.concatenate(split(own), axis=0)
     for i in range(CHUNKS):
@@ -102,9 +103,9 @@
     high_ref[rows:, :] = jnp.concatenate([high] * 4 + [low] * 4, axis=0)
 
 
-def product_kernel(block_ref, high_ref, low_ref, out_ref):
-    columns = high_ref.shape[1]
-    tiles = [unpacked(block_ref[j], block_ref[j + 1]) for j in range(0, columns // OWN, 2)]
+def product_kernel(*refs):
+    *blocks, high_ref, low_ref, out_ref = refs
+    tiles = [unpacked(block[j], block[j + 1]) for block in blocks for j in range(0, block.shape[0], 2)]
     panel = jnp.concatenate(split(jnp.concatenate(tiles, axis=1)), axis=0)
     rows = low_ref.shape[0]
     first = nt(panel, high_ref[...])
@@ -146,28 +147,28 @@
     peers = X * Y * C
     pieces = pl.pallas_call(pack_kernel, out_shape=jax.ShapeDtypeStruct((peers, 8, 128), f32), in_specs=[VMEM], out_specs=VMEM, compiler_params=SMALL, name="pack")(panel_t)
     slab = lax.all_to_all(pieces, PLANE, 0, 0, tiled=True)
-    block = lax.ppermute(slab, AXES, plane_to_column())
-    x_index = lax.axis_index("x").reshape(1)
+    pairs = plane_to_column()
+    blocks = [lax.ppermute(part, AXES, pairs) for part in jnp.split(slab, PARTS)]
     high, low = pl.pallas_call(
         prepare_kernel,
         out_shape=(
             jax.ShapeDtypeStruct((slab_rows + 8 * TRAITS, kinship.shape[1]), jnp.bfloat16),
             jax.ShapeDtypeStruct(kinship.shape, jnp.bfloat16),
         ),
-        in_specs=[pl.BlockSpec(memory_space=pltpu.SMEM), VMEM, pl.BlockSpec(memory_space=pltpu.HBM)],
+        in_specs=[VMEM, pl.BlockSpec(memory_space=pltpu.HBM)],
         out_specs=(VMEM, VMEM),
         scratch_shapes=[pltpu.VMEM((CHUNKS, slab_rows // CHUNKS, kinship.shape[1]), f32), pltpu.SemaphoreType.DMA((CHUNKS,))],
         compiler_params=WHOLE,
         name="prepare",
-    )(x_index, slab, kinship)
+    )(slab, kinship)
     parts = pl.pallas_call(
         product_kernel,
         out_shape=jax.ShapeDtypeStruct((Y * C, 16, 128), f32),
-        in_specs=[VMEM, VMEM, VMEM],
+        in_specs=[VMEM] * (PARTS + 2),
         out_specs=VMEM,
         compiler_params=LARGE,
         name="product",
-    )(block, high, low)
+    )(*blocks, high, low)
     parts = lax.all_to_all(parts, COLS, 0, 0, tiled=True)
     own, scores = pl.pallas_call(
         own_kernel,

time: 55.3 us -> 55.5 us (level)
  blocking collectives: 41 us -> 38.4 us
  waiting for transfers between devices: 0.18 us -> 1.8 us
  starting transfers between devices: 7.19 us -> 8.23 us
    all_to_all x1, blocking collectives: 16.1 us -> 12.1 us  [shards(): scores = lax.all_to_all(scores, ROWS, 0, 0, tiled=True)]
    ppermute x1 -> x2, waiting for transfers between devices: 0.18 us -> 1.8 us  [shards(): lax.ppermute(part, AXES, pairs)]
    all_to_all x1, blocking collectives: 8.86 us -> 10.3 us  [shards(): parts = lax.all_to_all(parts, COLS, 0, 0, tiled=True)]
    ppermute x1 -> x2, starting transfers between devices: 7.19 us -> 8.23 us  [shards(): lax.ppermute(part, AXES, pairs)]
  transfers between devices with their start and end apart: 1 -> 2, of which waited for: 1 -> 1; matrix products, arithmetic and copies ran while one was open for 0% -> 0% of each run, Pallas kernels for 6% -> 5%
where the time goes in v8:
time: 55.5 us; the launch traced here: 55.2 us
  blocking collectives  38.4 us (69%)
  starting transfers between devices  8.23 us (15%)
  Pallas kernels  5.36 us (10%)
  waiting for transfers between devices  1.8 us (3%)
  local copies, waits for them, and re-layouts  0.7 us (1%)
  between operations  0.66 us (1%)
    all_to_all x1, blocking collectives, shards(): slab = lax.all_to_all(pieces, PLANE, 0, 0, tiled=True)  16 us
    all_to_all x1, blocking collectives, shards(): scores = lax.all_to_all(scores, ROWS, 0, 0, tiled=True)  12.1 us
    all_to_all x1, blocking collectives, shards(): parts = lax.all_to_all(parts, COLS, 0, 0, tiled=True)  10.3 us
    ppermute x2, starting transfers between devices, shards(): lax.ppermute(part, AXES, pairs)  8.23 us
    pallas_call x1, Pallas kernels, shards(): pl.pallas_call(prepare_kernel, out_shape=(jax.ShapeDtypeStruct((slab_rows...  3.02 us
    ppermute x2, waiting for transfers between devices, shards(): lax.ppermute(part, AXES, pairs)  1.8 us
    pallas_call x1, Pallas kernels, shards(): pl.pallas_call(product_kernel, out_shape=jax.ShapeDtypeStruct((Y * C, 16,...  1.46 us
  transfers between devices with their start and end apart: 2, of which 1 were waited for; matrix products, arithmetic and copies ran while one was open for 0% of the time, Pallas kernels for 5%

profile of v8, /device:TPU:1, one launch (start us, length us, event | category | flops | bytes accessed | tf_op | source)
XLA Modules:
  0.0 55.2 jit_solution(3946314322496972884)
XLA Ops:
  0.6 0.0 copy-start
  0.6 0.7 %copy-done = f32[16,64]{1,0:T(8,128)S(1)} copy-done((f32[16,64]{1,0:T(8,128)S(1)}, f32[16,64]{1,0:T(8,128)}, u32[]{:S(2)}) %copy-start) | copy-done | bytes 4120
  1.3 0.1 pack.1
  1.4 16.0 %all_to_all.15.slab_ref = f32[32,8,128]{2,1,0:T(8,128)S(1)} all-to-all(f32[32,8,128]{2,1,0:T(8,128)S(1)} %pack.1), channel_id=1, replica_groups=mesh['z'=8,'x'=4,'y'=4,'c'=2] {'x','y','c'}, dimensions={0} | all-to-all | bytes 262144 | tf_op jit(solution)/shard_map/all_to_all | solution.py:149
  17.5 7.3 %collective-permute-start.1 = (f32[16,8,128]{2,1,0:T(8,128)S(1)}, f32[16,8,128]{2,1,0:T(8,128)S(1)}, u32[]{:S(2)}, u32[]{:S(2)}) collective-permute-start(f32[16,8,128]{2,1,0:T(8,128)S(1)} %get-tuple-element.10), channel_id=1, source_target_pairs={{4,0},{5,32},{2,224},{3,64},{6,192},{7,96},{0,160},{1,128},{12,8},... | collective-permute-start | bytes 196616 | tf_op jit(solution)/shard_map/ppermute | solution.py:151
  24.7 1.0 %collective-permute-start = (f32[16,8,128]{2,1,0:T(8,128)S(1)}, f32[16,8,128]{2,1,0:T(8,128)S(1)}, u32[]{:S(2)}, u32[]{:S(2)}) collective-permute-start(f32[16,8,128]{2,1,0:T(8,128)S(1)} %get-tuple-element.11), channel_id=1, source_target_pairs={{4,0},{5,32},{2,224},{3,64},{6,192},{7,96},{0,160},{1,128},{12,8},... | collective-permute-start | bytes 196616 | tf_op jit(solution)/shard_map/ppermute | solution.py:151
  25.7 3.0 %prepare.1 = (bf16[640,2048]{1,0:T(8,128)(2,1)S(1)}, bf16[512,2048]{1,0:T(8,128)(2,1)S(1)}) custom-call(f32[32,8,128]{2,1,0:T(8,128)S(1)} %all_to_all.15.slab_ref, f32[512,2048]{1,0:T(8,128)} %kinship_ref.1), custom_call_target="tpu_custom_call" | custom-call | tf_op jit(solution)/shard_map/prepare/pallas_call | solution.py:152
  28.7 0.0 collective-permute-done.1.refs_1_
  28.7 1.8 %collective-permute-done.refs_0_ = f32[16,8,128]{2,1,0:T(8,128)S(1)} collective-permute-done((f32[16,8,128]{2,1,0:T(8,128)S(1)}, f32[16,8,128]{2,1,0:T(8,128)S(1)}, u32[]{:S(2)}, u32[]{:S(2)}) %collective-permute-start) | collective-permute-done | bytes 65568 | tf_op jit(solution)/shard_map/ppermute | solution.py:151
  30.5 1.5 %product.1 = f32[8,16,128]{2,1,0:T(8,128)S(1)} custom-call(f32[16,8,128]{2,1,0:T(8,128)S(1)} %collective-permute-done.refs_0_, f32[16,8,128]{2,1,0:T(8,128)S(1)} %collective-permute-done.1.refs_1_, bf16[640,2048]{1,0:T(8,128)(2,1)S(1)} %get-tuple-element.6.refs_2_, bf16[512,2048]{1,0:T(8,128)(2,1)S(1)} %get-tuple-element.7.refs_3_), custom_call_target="tpu_custom_call" | custom-call | tf_op jit(solution)/shard_map/product/pallas_call | solution.py:164
  32.0 10.3 %all_to_all.16.parts_ref = f32[8,16,128]{2,1,0:T(8,128)S(1)} all-to-all(f32[8,16,128]{2,1,0:T(8,128)S(1)} %product.1), channel_id=1, replica_groups=mesh['z'=8,'x'=4,'y'=4,'c'=2] {'y','c'}, dimensions={0} | all-to-all | bytes 131072 | tf_op jit(solution)/shard_map/all_to_all | solution.py:172
  42.4 12.1 %all_to_all.17.refs_1_ = f32[32,2,128]{2,1,0:T(2,128)S(1)} all-to-all(f32[32,2,128]{2,1,0:T(2,128)S(1)} %get-tuple-element.9), channel_id=1, replica_groups=mesh['z'=8,'x'=4,'y'=4,'c'=2] {'z','x'}, dimensions={0} | all-to-all | bytes 65536 | tf_op jit(solution)/shard_map/all_to_all | solution.py:181
  54.4 0.8 %result.1 = (f32[16,64]{1,0:T(8,128)}, f32[16,16]{1,0:T(8,128)}) custom-call(f32[8,128]{1,0:T(8,128)S(1)} %get-tuple-element.8.refs_0_, f32[32,2,128]{2,1,0:T(2,128)S(1)} %all_to_all.17.refs_1_), custom_call_target="tpu_custom_call" | custom-call | tf_op jit(solution)/shard_map/result/pallas_call | solution.py:183
  (2 shorter events, 0.0 us)
Async XLA Ops:
  0.6 0.7 %copy-start = (f32[16,64]{1,0:T(8,128)S(1)}, f32[16,64]{1,0:T(8,128)}, u32[]{:S(2)}) copy-start(f32[16,64]{1,0:T(8,128)} %panel_ref.1) | copy-start | bytes 12292
  17.5 11.3 %collective-permute-start.1 = (f32[16,8,128]{2,1,0:T(8,128)S(1)}, f32[16,8,128]{2,1,0:T(8,128)S(1)}, u32[]{:S(2)}, u32[]{:S(2)}) collective-permute-start(f32[16,8,128]{2,1,0:T(8,128)S(1)} %get-tuple-element.10), channel_id=1, source_target_pairs={{4,0},{5,32},{2,224},{3,64},{6,192},{7,96},{0,160},{1,128},{12,8},... | collective-permute-start | bytes 196616 | tf_op jit(solution)/shard_map/ppermute | solution.py:151
  24.7 5.8 %collective-permute-start = (f32[16,8,128]{2,1,0:T(8,128)S(1)}, f32[16,8,128]{2,1,0:T(8,128)S(1)}, u32[]{:S(2)}, u32[]{:S(2)}) collective-permute-start(f32[16,8,128]{2,1,0:T(8,128)S(1)} %get-tuple-element.11), channel_id=1, source_target_pairs={{4,0},{5,32},{2,224},{3,64},{6,192},{7,96},{0,160},{1,128},{12,8},... | collective-permute-start | bytes 196616 | tf_op jit(solution)/shard_map/ppermute | solution.py:151

commit v9 on v3

--- a/solution.py
+++ b/solution.py
@@ -80,7 +80,7 @@
     out_ref[...] = jnp.broadcast_to(piece[None], out_ref.shape)
 
 
-def prepare_kernel(x_ref, slab_ref, kinship_ref, high_ref, low_ref, buffer, sems):
+def prepare_kernel(slab_ref, kinship_ref, high_ref, low_ref, buffer, sems):
     rows = kinship_ref.shape[0]
     height = rows // CHUNKS
 
@@ -89,7 +89,7 @@
 
     for i in range(CHUNKS):
         copy(i).start()
-    start = x_ref[0] * (Y * C)
+    start = lax.axis_index("x") * (Y * C)
     own = jnp.concatenate([unpacked(slab_ref[start + j], slab_ref[start + j + 1]) for j in range(0, Y * C, 2)], axis=1)
     own = jnp.concatenate(split(own), axis=0)
     for i in range(CHUNKS):
@@ -126,18 +126,20 @@
     wide = jnp.where(row == lane, wide, 0.0)
     top = jnp.sum(wide[:8], axis=0, keepdims=True)
     bottom = jnp.sum(wide[8:], axis=0, keepdims=True)
-    score = jnp.concatenate([top, bottom, jnp.zeros((6, 128), jnp.float32)], axis=0)
+    score = jnp.concatenate([top, bottom], axis=0)
     for y in range(Y):
         pair = packed(total[:, y * 128 : (y + 1) * 128])
         for c in range(C):
-            out_ref[y * C + c, :8, :] = pair[c]
-            out_ref[y * C + c, 8:, :] = score
+            for i in range(4):
+                out_ref[y * C + c, i] = pair[c][2 * i : 2 * i + 2]
+            out_ref[y * C + c, 4] = score
 
 
 def own_kernel(parts_ref, own_ref, score_ref):
     total = jnp.sum(parts_ref[...], axis=0)
-    own_ref[...] = total[:8]
-    score_ref[...] = jnp.broadcast_to(total[8:10][None], score_ref.shape)
+    for i in range(4):
+        own_ref[2 * i : 2 * i + 2, :] = total[i]
+    score_ref[...] = jnp.broadcast_to(total[4:], score_ref.shape)
 
 
 def result_kernel(own_ref, parts_ref, kin_ref, score_ref, *, scale):
@@ -158,19 +160,18 @@
     pairs = plane_to_column()
     early = lax.ppermute(slab[: peers // 2], AXES, pairs)
     late = lax.ppermute(slab[peers // 2 :], AXES, pairs)
-    x_index = lax.axis_index("x").reshape(1)
     high, low = pl.pallas_call(
         prepare_kernel,
         out_shape=(
             jax.ShapeDtypeStruct((slab_rows + 8 * TRAITS, kinship.shape[1]), jnp.bfloat16),
             jax.ShapeDtypeStruct(kinship.shape, jnp.bfloat16),
         ),
-        in_specs=[pl.BlockSpec(memory_space=pltpu.SMEM), VMEM, pl.BlockSpec(memory_space=pltpu.HBM)],
+        in_specs=[VMEM, pl.BlockSpec(memory_space=pltpu.HBM)],
         out_specs=(VMEM, VMEM),
         scratch_shapes=[pltpu.VMEM((CHUNKS, slab_rows // CHUNKS, kinship.shape[1]), f32), pltpu.SemaphoreType.DMA((CHUNKS,))],
         compiler_params=WHOLE,
         name="prepare",
-    )(x_index, slab, kinship)
+    )(slab, kinship)
     partial, wide = pl.pallas_call(
         first_kernel,
         out_shape=(jax.ShapeDtypeStruct((TRAITS, slab_rows), f32), jax.ShapeDtypeStruct((TRAITS, 8 * TRAITS), f32)),
@@ -181,7 +182,7 @@
     )(early, high, low)
     parts = pl.pallas_call(
         second_kernel,
-        out_shape=jax.ShapeDtypeStruct((Y * C, 16, 128), f32),
+        out_shape=jax.ShapeDtypeStruct((Y * C, 5, 2, 128), f32),
         in_specs=[VMEM] * 5,
         out_specs=VMEM,
         compiler_params=LARGE,

time: 54.9 us -> 54.8 us (level)
  no operation moved by 1% of the time
where the time goes in v9:
time: 54.8 us; the launch traced here: 54.5 us
  blocking collectives  38.4 us (70%)
  starting transfers between devices  8.23 us (15%)
  Pallas kernels  5.52 us (10%)
  waiting for transfers between devices  1.05 us (2%)
  local copies, waits for them, and re-layouts  0.7 us (1%)
  between operations  0.66 us (1%)
    all_to_all x1, blocking collectives, shards(): slab = lax.all_to_all(pieces, PLANE, 0, 0, tiled=True)  16 us
    all_to_all x1, blocking collectives, shards(): scores = lax.all_to_all(scores, ROWS, 0, 0, tiled=True)  12.1 us
    all_to_all x1, blocking collectives, shards(): parts = lax.all_to_all(parts, COLS, 0, 0, tiled=True)  10.2 us
    ppermute x1, starting transfers between devices, shards(): early = lax.ppermute(slab[:peers // 2], AXES, pairs)  7.28 us
    pallas_call x1, Pallas kernels, shards(): pl.pallas_call(prepare_kernel, out_shape=(jax.ShapeDtypeStruct((slab_rows...  3.02 us
  transfers between devices with their start and end apart: 2, of which 1 were waited for; matrix products, arithmetic and copies ran while one was open for 0% of the time, Pallas kernels for 7%

profile of v9, /device:TPU:1, one launch (start us, length us, event | category | flops | bytes accessed | tf_op | source)
XLA Modules:
  0.0 54.5 jit_solution(6341451188435184252)
XLA Ops:
  0.6 0.0 copy-start
  0.6 0.7 %copy-done = f32[16,64]{1,0:T(8,128)S(1)} copy-done((f32[16,64]{1,0:T(8,128)S(1)}, f32[16,64]{1,0:T(8,128)}, u32[]{:S(2)}) %copy-start) | copy-done | bytes 4120
  1.3 0.1 pack.1
  1.4 16.0 %all_to_all.15.slab_ref = f32[32,8,128]{2,1,0:T(8,128)S(1)} all-to-all(f32[32,8,128]{2,1,0:T(8,128)S(1)} %pack.1), channel_id=1, replica_groups=mesh['z'=8,'x'=4,'y'=4,'c'=2] {'x','y','c'}, dimensions={0} | all-to-all | bytes 262144 | tf_op jit(solution)/shard_map/all_to_all | solution.py:159
  17.5 7.3 %collective-permute-start.1 = (f32[16,8,128]{2,1,0:T(8,128)S(1)}, f32[16,8,128]{2,1,0:T(8,128)S(1)}, u32[]{:S(2)}, u32[]{:S(2)}) collective-permute-start(f32[16,8,128]{2,1,0:T(8,128)S(1)} %get-tuple-element.14), channel_id=1, source_target_pairs={{4,0},{5,32},{2,224},{3,64},{6,192},{7,96},{0,160},{1,128},{12,8},... | collective-permute-start | bytes 196616 | tf_op jit(solution)/shard_map/ppermute | solution.py:161
  24.7 1.0 %collective-permute-start = (f32[16,8,128]{2,1,0:T(8,128)S(1)}, f32[16,8,128]{2,1,0:T(8,128)S(1)}, u32[]{:S(2)}, u32[]{:S(2)}) collective-permute-start(f32[16,8,128]{2,1,0:T(8,128)S(1)} %get-tuple-element.15), channel_id=1, source_target_pairs={{4,0},{5,32},{2,224},{3,64},{6,192},{7,96},{0,160},{1,128},{12,8},... | collective-permute-start | bytes 196616 | tf_op jit(solution)/shard_map/ppermute | solution.py:162
  25.7 3.0 %prepare.1 = (bf16[640,2048]{1,0:T(8,128)(2,1)S(1)}, bf16[512,2048]{1,0:T(8,128)(2,1)S(1)}) custom-call(f32[32,8,128]{2,1,0:T(8,128)S(1)} %all_to_all.15.slab_ref, f32[512,2048]{1,0:T(8,128)} %kinship_ref.1), custom_call_target="tpu_custom_call" | custom-call | tf_op jit(solution)/shard_map/prepare/pallas_call | solution.py:163
  28.7 0.0 collective-permute-done.1.block_ref
  28.7 0.8 %first.1 = (f32[16,512]{1,0:T(8,128)S(1)}, f32[16,128]{1,0:T(8,128)S(1)}) custom-call(f32[16,8,128]{2,1,0:T(8,128)S(1)} %collective-permute-done.1.block_ref, bf16[640,2048]{1,0:T(8,128)(2,1)S(1)} %get-tuple-element.8.high_ref, bf16[512,2048]{1,0:T(8,128)(2,1)S(1)} %get-tuple-element.9.low_ref), custom_call_target="tpu_custom_call" | custom-call | tf_op jit(solution)/shard_map/first/pallas_call | solution.py:175
  29.5 1.0 %collective-permute-done.block_ref = f32[16,8,128]{2,1,0:T(8,128)S(1)} collective-permute-done((f32[16,8,128]{2,1,0:T(8,128)S(1)}, f32[16,8,128]{2,1,0:T(8,128)S(1)}, u32[]{:S(2)}, u32[]{:S(2)}) %collective-permute-start) | collective-permute-done | bytes 65568 | tf_op jit(solution)/shard_map/ppermute | solution.py:162
  30.5 0.9 %second.1 = f32[8,5,2,128]{3,2,1,0:T(2,128)S(1)} custom-call(f32[16,8,128]{2,1,0:T(8,128)S(1)} %collective-permute-done.block_ref, bf16[640,2048]{1,0:T(8,128)(2,1)S(1)} %get-tuple-element.8.high_ref, bf16[512,2048]{1,0:T(8,128)(2,1)S(1)} %get-tuple-element.9.low_ref, f32[16,512]{1,0:T(8,128)S(1)} %get-tuple-element.10.partial_ref, ...), custom_call_target="tpu_custom_call" | custom-call | tf_op jit(solution)/shard_map/second/pallas_call | solution.py:183
  31.4 10.2 %all_to_all.16.parts_ref = f32[8,5,2,128]{3,2,1,0:T(2,128)S(1)} all-to-all(f32[8,5,2,128]{3,2,1,0:T(2,128)S(1)} %second.1), channel_id=1, replica_groups=mesh['z'=8,'x'=4,'y'=4,'c'=2] {'y','c'}, dimensions={0} | all-to-all | bytes 81920 | tf_op jit(solution)/shard_map/all_to_all | solution.py:191
  41.7 12.1 %all_to_all.17.refs_1_ = f32[32,2,128]{2,1,0:T(2,128)S(1)} all-to-all(f32[32,2,128]{2,1,0:T(2,128)S(1)} %get-tuple-element.13), channel_id=1, replica_groups=mesh['z'=8,'x'=4,'y'=4,'c'=2] {'z','x'}, dimensions={0} | all-to-all | bytes 65536 | tf_op jit(solution)/shard_map/all_to_all | solution.py:200
  53.8 0.8 %result.1 = (f32[16,64]{1,0:T(8,128)}, f32[16,16]{1,0:T(8,128)}) custom-call(f32[8,128]{1,0:T(8,128)S(1)} %get-tuple-element.12.refs_0_, f32[32,2,128]{2,1,0:T(2,128)S(1)} %all_to_all.17.refs_1_), custom_call_target="tpu_custom_call" | custom-call | tf_op jit(solution)/shard_map/result/pallas_call | solution.py:202
  (2 shorter events, 0.0 us)
Async XLA Ops:
  0.6 0.7 %copy-start = (f32[16,64]{1,0:T(8,128)S(1)}, f32[16,64]{1,0:T(8,128)}, u32[]{:S(2)}) copy-start(f32[16,64]{1,0:T(8,128)} %panel_ref.1) | copy-start | bytes 12292
  17.5 11.3 %collective-permute-start.1 = (f32[16,8,128]{2,1,0:T(8,128)S(1)}, f32[16,8,128]{2,1,0:T(8,128)S(1)}, u32[]{:S(2)}, u32[]{:S(2)}) collective-permute-start(f32[16,8,128]{2,1,0:T(8,128)S(1)} %get-tuple-element.14), channel_id=1, source_target_pairs={{4,0},{5,32},{2,224},{3,64},{6,192},{7,96},{0,160},{1,128},{12,8},... | collective-permute-start | bytes 196616 | tf_op jit(solution)/shard_map/ppermute | solution.py:161
  24.7 5.8 %collective-permute-start = (f32[16,8,128]{2,1,0:T(8,128)S(1)}, f32[16,8,128]{2,1,0:T(8,128)S(1)}, u32[]{:S(2)}, u32[]{:S(2)}) collective-permute-start(f32[16,8,128]{2,1,0:T(8,128)S(1)} %get-tuple-element.15), channel_id=1, source_target_pairs={{4,0},{5,32},{2,224},{3,64},{6,192},{7,96},{0,160},{1,128},{12,8},... | collective-permute-start | bytes 196616 | tf_op jit(solution)/shard_map/ppermute | solution.py:162

commit v10 on v9

--- a/solution.py
+++ b/solution.py
@@ -15,7 +15,7 @@
 PLANE = ("x", "y", "c")
 TRAITS = 16
 OWN = 64
-CHUNKS = 8
+CHUNKS = 4
 HALF = 64
 VMEM = pl.BlockSpec(memory_space=pltpu.VMEM)
 SMALL = pltpu.CompilerParams(vmem_limit_bytes=2 << 20)
@@ -66,10 +66,6 @@
     return high, (x - high.astype(jnp.float32)).astype(jnp.bfloat16)
 
 
-def nt(left, right):
-    return lax.dot_general(left, right, (((1,), (1,)), ((), ())), preferred_element_type=jnp.float32)
-
-
 def nn(left, right):
     return lax.dot_general(left, right, (((1,), (0,)), ((), ())), preferred_element_type=jnp.float32)
 
@@ -92,23 +88,25 @@
     start = lax.axis_index("x") * (Y * C)
     own = jnp.concatenate([unpacked(slab_ref[start + j], slab_ref[start + j + 1]) for j in range(0, Y * C, 2)], axis=1)
     own = jnp.concatenate(split(own), axis=0)
+    form = jnp.zeros((2 * TRAITS, kinship_ref.shape[1]), jnp.float32)
     for i in range(CHUNKS):
         copy(i).wait()
-        high, low = split(buffer[i])
-        high_ref[pl.ds(i * height, height), :] = high
-        low_ref[pl.ds(i * height, height), :] = low
-    form = nn(own, high_ref[:rows, :]) + nn(own, low_ref[:rows, :])
-    high, low = split(form[:TRAITS] + form[TRAITS:])
-    high_ref[rows:, :] = jnp.concatenate([high] * 4 + [low] * 4, axis=0)
+        across = slice(i * height, (i + 1) * height)
+        high_ref[:, across], low_ref[:, across] = split(buffer[i].T)
+        for part in split(buffer[i]):
+            form = form + nn(own[:, across], part)
+    form = form[:TRAITS] + form[TRAITS:]
+    high, low = (part.astype(jnp.float32) for part in split(form))
+    high_ref[:, rows:] = jnp.concatenate([high] * 4 + [low] * 4, axis=0).T.astype(jnp.bfloat16)
 
 
 def half_product(block_ref, high_ref, low_ref, start):
     columns = block_ref.shape[0] * OWN
     tiles = [unpacked(block_ref[j], block_ref[j + 1]) for j in range(0, block_ref.shape[0], 2)]
     panel = jnp.concatenate(split(jnp.concatenate(tiles, axis=1)), axis=0)
-    rows = low_ref.shape[0]
-    both = nt(panel, high_ref[:, start : start + columns])
-    partial = both[:, :rows] + nt(panel, low_ref[:, start : start + columns])
+    rows = low_ref.shape[1]
+    both = nn(panel, high_ref[start : start + columns, :])
+    partial = both[:, :rows] + nn(panel, low_ref[start : start + columns, :])
     return partial[:TRAITS] + partial[TRAITS:], both[:TRAITS, rows:] + both[TRAITS:, rows:]
 
 
@@ -163,8 +161,8 @@
     high, low = pl.pallas_call(
         prepare_kernel,
         out_shape=(
-            jax.ShapeDtypeStruct((slab_rows + 8 * TRAITS, kinship.shape[1]), jnp.bfloat16),
-            jax.ShapeDtypeStruct(kinship.shape, jnp.bfloat16),
+            jax.ShapeDtypeStruct((kinship.shape[1], slab_rows + 8 * TRAITS), jnp.bfloat16),
+            jax.ShapeDtypeStruct(kinship.shape[::-1], jnp.bfloat16),
         ),
         in_specs=[VMEM, pl.BlockSpec(memory_space=pltpu.HBM)],
         out_specs=(VMEM, VMEM),

time: 54.8 us -> 54.5 us (level)
  no operation moved by 1% of the time
where the time goes in v10:
time: 54.5 us; the launch traced here: 54.2 us
  blocking collectives  38.3 us (70%)
  starting transfers between devices  8.23 us (15%)
  Pallas kernels  5.04 us (9%)
  waiting for transfers between devices  1.26 us (2%)
  local copies, waits for them, and re-layouts  0.7 us (1%)
  between operations  0.66 us (1%)
    all_to_all x1, blocking collectives, shards(): slab = lax.all_to_all(pieces, PLANE, 0, 0, tiled=True)  16 us
    all_to_all x1, blocking collectives, shards(): scores = lax.all_to_all(scores, ROWS, 0, 0, tiled=True)  12.1 us
    all_to_all x1, blocking collectives, shards(): parts = lax.all_to_all(parts, COLS, 0, 0, tiled=True)  10.2 us
    ppermute x1, starting transfers between devices, shards(): early = lax.ppermute(slab[:peers // 2], AXES, pairs)  7.28 us
    pallas_call x1, Pallas kernels, shards(): pl.pallas_call(prepare_kernel, out_shape=(jax.ShapeDtypeStruct((kinship.s...  3.05 us
    ppermute x1, waiting for transfers between devices, shards(): late = lax.ppermute(slab[peers // 2:], AXES, pairs)  1.26 us
  transfers between devices with their start and end apart: 2, of which 1 were waited for; matrix products, arithmetic and copies ran while one was open for 0% of the time, Pallas kernels for 7%

profile of v10, /device:TPU:1, one launch (start us, length us, event | category | flops | bytes accessed | tf_op | source)
XLA Modules:
  0.0 54.2 jit_solution(17149177330238179804)
XLA Ops:
  0.6 0.0 copy-start
  0.6 0.7 %copy-done = f32[16,64]{1,0:T(8,128)S(1)} copy-done((f32[16,64]{1,0:T(8,128)S(1)}, f32[16,64]{1,0:T(8,128)}, u32[]{:S(2)}) %copy-start) | copy-done | bytes 4120
  1.3 0.1 pack.1
  1.4 16.0 %all_to_all.15.slab_ref = f32[32,8,128]{2,1,0:T(8,128)S(1)} all-to-all(f32[32,8,128]{2,1,0:T(8,128)S(1)} %pack.1), channel_id=1, replica_groups=mesh['z'=8,'x'=4,'y'=4,'c'=2] {'x','y','c'}, dimensions={0} | all-to-all | bytes 262144 | tf_op jit(solution)/shard_map/all_to_all | solution.py:157
  17.5 7.3 %collective-permute-start.1 = (f32[16,8,128]{2,1,0:T(8,128)S(1)}, f32[16,8,128]{2,1,0:T(8,128)S(1)}, u32[]{:S(2)}, u32[]{:S(2)}) collective-permute-start(f32[16,8,128]{2,1,0:T(8,128)S(1)} %get-tuple-element.14), channel_id=1, source_target_pairs={{4,0},{5,32},{2,224},{3,64},{6,192},{7,96},{0,160},{1,128},{12,8},... | collective-permute-start | bytes 196616 | tf_op jit(solution)/shard_map/ppermute | solution.py:159
  24.7 1.0 %collective-permute-start = (f32[16,8,128]{2,1,0:T(8,128)S(1)}, f32[16,8,128]{2,1,0:T(8,128)S(1)}, u32[]{:S(2)}, u32[]{:S(2)}) collective-permute-start(f32[16,8,128]{2,1,0:T(8,128)S(1)} %get-tuple-element.15), channel_id=1, source_target_pairs={{4,0},{5,32},{2,224},{3,64},{6,192},{7,96},{0,160},{1,128},{12,8},... | collective-permute-start | bytes 196616 | tf_op jit(solution)/shard_map/ppermute | solution.py:160
  25.7 3.0 %prepare.1 = (bf16[2048,640]{1,0:T(8,128)(2,1)S(1)}, bf16[2048,512]{1,0:T(8,128)(2,1)S(1)}) custom-call(f32[32,8,128]{2,1,0:T(8,128)S(1)} %all_to_all.15.slab_ref, f32[512,2048]{1,0:T(8,128)} %kinship_ref.1), custom_call_target="tpu_custom_call" | custom-call | tf_op jit(solution)/shard_map/prepare/pallas_call | solution.py:161
  28.8 0.0 collective-permute-done.1.block_ref
  28.8 0.5 first.1
  29.3 1.3 %collective-permute-done.block_ref = f32[16,8,128]{2,1,0:T(8,128)S(1)} collective-permute-done((f32[16,8,128]{2,1,0:T(8,128)S(1)}, f32[16,8,128]{2,1,0:T(8,128)S(1)}, u32[]{:S(2)}, u32[]{:S(2)}) %collective-permute-start) | collective-permute-done | bytes 65568 | tf_op jit(solution)/shard_map/ppermute | solution.py:160
  30.5 0.6 %second.1 = f32[8,5,2,128]{3,2,1,0:T(2,128)S(1)} custom-call(f32[16,8,128]{2,1,0:T(8,128)S(1)} %collective-permute-done.block_ref, bf16[2048,640]{1,0:T(8,128)(2,1)S(1)} %get-tuple-element.8.high_ref, bf16[2048,512]{1,0:T(8,128)(2,1)S(1)} %get-tuple-element.9.low_ref, f32[16,512]{1,0:T(8,128)S(1)} %get-tuple-element.10.partial_ref, ...), custom_call_target="tpu_custom_call" | custom-call | tf_op jit(solution)/shard_map/second/pallas_call | solution.py:181
  31.1 10.2 %all_to_all.16.parts_ref = f32[8,5,2,128]{3,2,1,0:T(2,128)S(1)} all-to-all(f32[8,5,2,128]{3,2,1,0:T(2,128)S(1)} %second.1), channel_id=1, replica_groups=mesh['z'=8,'x'=4,'y'=4,'c'=2] {'y','c'}, dimensions={0} | all-to-all | bytes 81920 | tf_op jit(solution)/shard_map/all_to_all | solution.py:189
  41.4 12.1 %all_to_all.17.refs_1_ = f32[32,2,128]{2,1,0:T(2,128)S(1)} all-to-all(f32[32,2,128]{2,1,0:T(2,128)S(1)} %get-tuple-element.13), channel_id=1, replica_groups=mesh['z'=8,'x'=4,'y'=4,'c'=2] {'z','x'}, dimensions={0} | all-to-all | bytes 65536 | tf_op jit(solution)/shard_map/all_to_all | solution.py:198
  53.4 0.8 %result.1 = (f32[16,64]{1,0:T(8,128)}, f32[16,16]{1,0:T(8,128)}) custom-call(f32[8,128]{1,0:T(8,128)S(1)} %get-tuple-element.12.refs_0_, f32[32,2,128]{2,1,0:T(2,128)S(1)} %all_to_all.17.refs_1_), custom_call_target="tpu_custom_call" | custom-call | tf_op jit(solution)/shard_map/result/pallas_call | solution.py:200
  (2 shorter events, 0.0 us)
Async XLA Ops:
  0.6 0.7 %copy-start = (f32[16,64]{1,0:T(8,128)S(1)}, f32[16,64]{1,0:T(8,128)}, u32[]{:S(2)}) copy-start(f32[16,64]{1,0:T(8,128)} %panel_ref.1) | copy-start | bytes 12292
  17.5 11.3 %collective-permute-start.1 = (f32[16,8,128]{2,1,0:T(8,128)S(1)}, f32[16,8,128]{2,1,0:T(8,128)S(1)}, u32[]{:S(2)}, u32[]{:S(2)}) collective-permute-start(f32[16,8,128]{2,1,0:T(8,128)S(1)} %get-tuple-element.14), channel_id=1, source_target_pairs={{4,0},{5,32},{2,224},{3,64},{6,192},{7,96},{0,160},{1,128},{12,8},... | collective-permute-start | bytes 196616 | tf_op jit(solution)/shard_map/ppermute | solution.py:159
  24.7 5.8 %collective-permute-start = (f32[16,8,128]{2,1,0:T(8,128)S(1)}, f32[16,8,128]{2,1,0:T(8,128)S(1)}, u32[]{:S(2)}, u32[]{:S(2)}) collective-permute-start(f32[16,8,128]{2,1,0:T(8,128)S(1)} %get-tuple-element.15), channel_id=1, source_target_pairs={{4,0},{5,32},{2,224},{3,64},{6,192},{7,96},{0,160},{1,128},{12,8},... | collective-permute-start | bytes 196616 | tf_op jit(solution)/shard_map/ppermute | solution.py:160

commit v11 on v10

--- a/solution.py
+++ b/solution.py
@@ -1,5 +1,3 @@
-import itertools
-
 import jax
 import jax.numpy as jnp
 from jax import lax
@@ -27,21 +25,22 @@
     return ((z * X + x) * Y + y) * C + c
 
 
-def apart(a, b, n):
-    d = abs(a - b) % n
-    return min(d, n - d)
+SENDER = (
+    (6, 2, 5, 0, 1, 3, 7, 4),
+    (5, 4, 3, 2, 7, 0, 1, 6),
+    (0, 6, 1, 7, 4, 2, 3, 5),
+    (2, 1, 6, 5, 7, 4, 0, 3),
+    (4, 7, 2, 1, 3, 0, 6, 5),
+    (7, 5, 4, 2, 0, 6, 3, 1),
+    (3, 0, 7, 1, 4, 2, 5, 6),
+    (0, 2, 5, 6, 7, 4, 3, 1),
+)
 
 
 def plane_to_column():
-    pairs = []
-    for plane in range(Z):
-        y_to, c_to = divmod(plane, C)
-        senders = sorted(itertools.product(range(Y), range(C)), key=lambda s: (-apart(s[0], y_to, Y), (s[0] - y_to) % Y, s[1] != c_to))
-        planes = sorted(range(Z), key=lambda z: (apart(z, plane, Z), (z - plane) % Z))
-        for x in range(X):
-            for (y, c), z in zip(senders, planes):
-                pairs.append((number(plane, x, y, c), number(z, x, y_to, c_to)))
-    return pairs
+    return [
+        (number(p, x, *divmod(SENDER[p][z], C)), number(z, x, *divmod(p, C))) for p in range(Z) for x in range(X) for z in range(Z)
+    ]
 
 
 def low_lanes(shape):

time: 54.5 us -> 55.4 us (1.017)
  blocking collectives: 38.3 us -> 39.3 us
    all_to_all x1, blocking collectives: 12.1 us -> 12.8 us  [shards(): scores = lax.all_to_all(scores, ROWS, 0, 0, tiled=True)]
  transfers between devices with their start and end apart: 2 -> 2, of which waited for: 1 -> 1; matrix products, arithmetic and copies ran while one was open for 0% -> 0% of each run, Pallas kernels for 7% -> 6%
where the time goes in v11:
time: 55.4 us; the launch traced here: 55.1 us
  blocking collectives  39.3 us (71%)
  starting transfers between devices  8.69 us (16%)
  Pallas kernels  5.04 us (9%)
  waiting for transfers between devices  0.75 us (1%)
  local copies, waits for them, and re-layouts  0.7 us (1%)
  between operations  0.66 us (1%)
    all_to_all x1, blocking collectives, shards(): slab = lax.all_to_all(pieces, PLANE, 0, 0, tiled=True)  16 us
    all_to_all x1, blocking collectives, shards(): scores = lax.all_to_all(scores, ROWS, 0, 0, tiled=True)  12.8 us
    all_to_all x1, blocking collectives, shards(): parts = lax.all_to_all(parts, COLS, 0, 0, tiled=True)  10.4 us
    ppermute x1, starting transfers between devices, shards(): early = lax.ppermute(slab[:peers // 2], AXES, pairs)  7.28 us
    pallas_call x1, Pallas kernels, shards(): pl.pallas_call(prepare_kernel, out_shape=(jax.ShapeDtypeStruct((kinship.s...  3.05 us
    ppermute x1, starting transfers between devices, shards(): late = lax.ppermute(slab[peers // 2:], AXES, pairs)  1.41 us
  transfers between devices with their start and end apart: 2, of which 1 were waited for; matrix products, arithmetic and copies ran while one was open for 0% of the time, Pallas kernels for 6%

profile of v11, /device:TPU:1, one launch (start us, length us, event | category | flops | bytes accessed | tf_op | source)
XLA Modules:
  0.0 55.1 jit_solution(8495501281243539467)
XLA Ops:
  0.6 0.0 copy-start
  0.6 0.7 %copy-done = f32[16,64]{1,0:T(8,128)S(1)} copy-done((f32[16,64]{1,0:T(8,128)S(1)}, f32[16,64]{1,0:T(8,128)}, u32[]{:S(2)}) %copy-start) | copy-done | bytes 4120
  1.3 0.1 pack.1
  1.4 16.0 %all_to_all.15.slab_ref = f32[32,8,128]{2,1,0:T(8,128)S(1)} all-to-all(f32[32,8,128]{2,1,0:T(8,128)S(1)} %pack.1), channel_id=1, replica_groups=mesh['z'=8,'x'=4,'y'=4,'c'=2] {'x','y','c'}, dimensions={0} | all-to-all | bytes 262144 | tf_op jit(solution)/shard_map/all_to_all | solution.py:156
  17.5 7.3 %collective-permute-start.1 = (f32[16,8,128]{2,1,0:T(8,128)S(1)}, f32[16,8,128]{2,1,0:T(8,128)S(1)}, u32[]{:S(2)}, u32[]{:S(2)}) collective-permute-start(f32[16,8,128]{2,1,0:T(8,128)S(1)} %get-tuple-element.14), channel_id=1, source_target_pairs={{6,0},{2,32},{5,64},{0,96},{1,128},{3,160},{7,192},{4,224},{14,8},... | collective-permute-start | bytes 196616 | tf_op jit(solution)/shard_map/ppermute | solution.py:158
  24.7 1.4 %collective-permute-start = (f32[16,8,128]{2,1,0:T(8,128)S(1)}, f32[16,8,128]{2,1,0:T(8,128)S(1)}, u32[]{:S(2)}, u32[]{:S(2)}) collective-permute-start(f32[16,8,128]{2,1,0:T(8,128)S(1)} %get-tuple-element.15), channel_id=1, source_target_pairs={{6,0},{2,32},{5,64},{0,96},{1,128},{3,160},{7,192},{4,224},{14,8},... | collective-permute-start | bytes 196616 | tf_op jit(solution)/shard_map/ppermute | solution.py:159
  26.2 3.0 %prepare.1 = (bf16[2048,640]{1,0:T(8,128)(2,1)S(1)}, bf16[2048,512]{1,0:T(8,128)(2,1)S(1)}) custom-call(f32[32,8,128]{2,1,0:T(8,128)S(1)} %all_to_all.15.slab_ref, f32[512,2048]{1,0:T(8,128)} %kinship_ref.1), custom_call_target="tpu_custom_call" | custom-call | tf_op jit(solution)/shard_map/prepare/pallas_call | solution.py:160
  29.2 0.0 collective-permute-done.1.block_ref
  29.2 0.5 first.1
  29.7 0.8 %collective-permute-done.block_ref = f32[16,8,128]{2,1,0:T(8,128)S(1)} collective-permute-done((f32[16,8,128]{2,1,0:T(8,128)S(1)}, f32[16,8,128]{2,1,0:T(8,128)S(1)}, u32[]{:S(2)}, u32[]{:S(2)}) %collective-permute-start) | collective-permute-done | bytes 65568 | tf_op jit(solution)/shard_map/ppermute | solution.py:159
  30.5 0.6 %second.1 = f32[8,5,2,128]{3,2,1,0:T(2,128)S(1)} custom-call(f32[16,8,128]{2,1,0:T(8,128)S(1)} %collective-permute-done.block_ref, bf16[2048,640]{1,0:T(8,128)(2,1)S(1)} %get-tuple-element.8.high_ref, bf16[2048,512]{1,0:T(8,128)(2,1)S(1)} %get-tuple-element.9.low_ref, f32[16,512]{1,0:T(8,128)S(1)} %get-tuple-element.10.partial_ref, ...), custom_call_target="tpu_custom_call" | custom-call | tf_op jit(solution)/shard_map/second/pallas_call | solution.py:180
  31.1 10.4 %all_to_all.16.parts_ref = f32[8,5,2,128]{3,2,1,0:T(2,128)S(1)} all-to-all(f32[8,5,2,128]{3,2,1,0:T(2,128)S(1)} %second.1), channel_id=1, replica_groups=mesh['z'=8,'x'=4,'y'=4,'c'=2] {'y','c'}, dimensions={0} | all-to-all | bytes 81920 | tf_op jit(solution)/shard_map/all_to_all | solution.py:188
  41.5 12.8 %all_to_all.17.refs_1_ = f32[32,2,128]{2,1,0:T(2,128)S(1)} all-to-all(f32[32,2,128]{2,1,0:T(2,128)S(1)} %get-tuple-element.13), channel_id=1, replica_groups=mesh['z'=8,'x'=4,'y'=4,'c'=2] {'z','x'}, dimensions={0} | all-to-all | bytes 65536 | tf_op jit(solution)/shard_map/all_to_all | solution.py:197
  54.3 0.8 %result.1 = (f32[16,64]{1,0:T(8,128)}, f32[16,16]{1,0:T(8,128)}) custom-call(f32[8,128]{1,0:T(8,128)S(1)} %get-tuple-element.12.refs_0_, f32[32,2,128]{2,1,0:T(2,128)S(1)} %all_to_all.17.refs_1_), custom_call_target="tpu_custom_call" | custom-call | tf_op jit(solution)/shard_map/result/pallas_call | solution.py:199
  (2 shorter events, 0.0 us)
Async XLA Ops:
  0.6 0.7 %copy-start = (f32[16,64]{1,0:T(8,128)S(1)}, f32[16,64]{1,0:T(8,128)}, u32[]{:S(2)}) copy-start(f32[16,64]{1,0:T(8,128)} %panel_ref.1) | copy-start | bytes 12292
  17.5 11.7 %collective-permute-start.1 = (f32[16,8,128]{2,1,0:T(8,128)S(1)}, f32[16,8,128]{2,1,0:T(8,128)S(1)}, u32[]{:S(2)}, u32[]{:S(2)}) collective-permute-start(f32[16,8,128]{2,1,0:T(8,128)S(1)} %get-tuple-element.14), channel_id=1, source_target_pairs={{6,0},{2,32},{5,64},{0,96},{1,128},{3,160},{7,192},{4,224},{14,8},... | collective-permute-start | bytes 196616 | tf_op jit(solution)/shard_map/ppermute | solution.py:158
  24.7 5.7 %collective-permute-start = (f32[16,8,128]{2,1,0:T(8,128)S(1)}, f32[16,8,128]{2,1,0:T(8,128)S(1)}, u32[]{:S(2)}, u32[]{:S(2)}) collective-permute-start(f32[16,8,128]{2,1,0:T(8,128)S(1)} %get-tuple-element.15), channel_id=1, source_target_pairs={{6,0},{2,32},{5,64},{0,96},{1,128},{3,160},{7,192},{4,224},{14,8},... | collective-permute-start | bytes 196616 | tf_op jit(solution)/shard_map/ppermute | solution.py:159

commit v12 on v11

--- a/solution.py
+++ b/solution.py
@@ -99,24 +99,14 @@
     high_ref[:, rows:] = jnp.concatenate([high] * 4 + [low] * 4, axis=0).T.astype(jnp.bfloat16)
 
 
-def half_product(block_ref, high_ref, low_ref, start):
-    columns = block_ref.shape[0] * OWN
+def product_kernel(block_ref, high_ref, low_ref, out_ref):
     tiles = [unpacked(block_ref[j], block_ref[j + 1]) for j in range(0, block_ref.shape[0], 2)]
     panel = jnp.concatenate(split(jnp.concatenate(tiles, axis=1)), axis=0)
     rows = low_ref.shape[1]
-    both = nn(panel, high_ref[start : start + columns, :])
-    partial = both[:, :rows] + nn(panel, low_ref[start : start + columns, :])
-    return partial[:TRAITS] + partial[TRAITS:], both[:TRAITS, rows:] + both[TRAITS:, rows:]
-
-
-def first_kernel(block_ref, high_ref, low_ref, partial_ref, wide_ref):
-    partial_ref[...], wide_ref[...] = half_product(block_ref, high_ref, low_ref, 0)
-
-
-def second_kernel(block_ref, high_ref, low_ref, partial_ref, wide_ref, out_ref):
-    total, wide = half_product(block_ref, high_ref, low_ref, block_ref.shape[0] * OWN)
-    total = total + partial_ref[...]
-    wide = wide + wide_ref[...]
+    both = nn(panel, high_ref[...])
+    total = both[:, :rows] + nn(panel, low_ref[...])
+    total = total[:TRAITS] + total[TRAITS:]
+    wide = both[:TRAITS, rows:] + both[TRAITS:, rows:]
     wide = wide + pltpu.roll(wide, HALF, 1)
     row = lax.broadcasted_iota(jnp.int32, wide.shape, 0) % 8
     lane = lax.broadcasted_iota(jnp.int32, wide.shape, 1) // TRAITS
@@ -154,9 +144,7 @@
     peers = X * Y * C
     pieces = pl.pallas_call(pack_kernel, out_shape=jax.ShapeDtypeStruct((peers, 8, 128), f32), in_specs=[VMEM], out_specs=VMEM, compiler_params=SMALL, name="pack")(panel_t)
     slab = lax.all_to_all(pieces, PLANE, 0, 0, tiled=True)
-    pairs = plane_to_column()
-    early = lax.ppermute(slab[: peers // 2], AXES, pairs)
-    late = lax.ppermute(slab[peers // 2 :], AXES, pairs)
+    block = lax.ppermute(slab, AXES, plane_to_column())
     high, low = pl.pallas_call(
         prepare_kernel,
         out_shape=(
@@ -169,22 +157,14 @@
         compiler_params=WHOLE,
         name="prepare",
     )(slab, kinship)
-    partial, wide = pl.pallas_call(
-        first_kernel,
-        out_shape=(jax.ShapeDtypeStruct((TRAITS, slab_rows), f32), jax.ShapeDtypeStruct((TRAITS, 8 * TRAITS), f32)),
-        in_specs=[VMEM, VMEM, VMEM],
-        out_specs=(VMEM, VMEM),
-        compiler_params=LARGE,
-        name="first",
-    )(early, high, low)
     parts = pl.pallas_call(
-        second_kernel,
+        product_kernel,
         out_shape=jax.ShapeDtypeStruct((Y * C, 5, 2, 128), f32),
-        in_specs=[VMEM] * 5,
+        in_specs=[VMEM] * 3,
         out_specs=VMEM,
         compiler_params=LARGE,
-        name="second",
-    )(late, high, low, partial, wide)
+        name="product",
+    )(block, high, low)
     parts = lax.all_to_all(parts, COLS, 0, 0, tiled=True)
     own, scores = pl.pallas_call(
         own_kernel,

time: 55.4 us -> 54 us (0.975)
  starting transfers between devices: 8.69 us -> 7.19 us
  blocking collectives: 39.3 us -> 40.3 us
  waiting for transfers between devices: 0.75 us -> 0.01 us
    all_to_all x1, blocking collectives: 12.8 us -> 15.6 us  [shards(): scores = lax.all_to_all(scores, ROWS, 0, 0, tiled=True)]
    all_to_all x1, blocking collectives: 10.4 us -> 8.71 us  [shards(): parts = lax.all_to_all(parts, COLS, 0, 0, tiled=True)]
    ppermute x2 -> x1, starting transfers between devices: 8.69 us -> 7.19 us  [shards(): block = lax.ppermute(slab, AXES, plane_to_column())]
    ppermute x2 -> x1, waiting for transfers between devices: 0.75 us -> 0.01 us  [shards(): block = lax.ppermute(slab, AXES, plane_to_column())]
  transfers between devices with their start and end apart: 2 -> 1, of which waited for: 1 -> 0; matrix products, arithmetic and copies ran while one was open for 0% -> 0% of each run, Pallas kernels for 6% -> 6%
where the time goes in v12:
time: 54 us; the launch traced here: 53.8 us
  blocking collectives  40.3 us (75%)
  starting transfers between devices  7.19 us (13%)
  Pallas kernels  4.9 us (9%)
  local copies, waits for them, and re-layouts  0.69 us (1%)
  between operations  0.66 us (1%)
    all_to_all x1, blocking collectives, shards(): slab = lax.all_to_all(pieces, PLANE, 0, 0, tiled=True)  16 us
    all_to_all x1, blocking collectives, shards(): scores = lax.all_to_all(scores, ROWS, 0, 0, tiled=True)  15.6 us
    all_to_all x1, blocking collectives, shards(): parts = lax.all_to_all(parts, COLS, 0, 0, tiled=True)  8.71 us
    ppermute x1, starting transfers between devices, shards(): block = lax.ppermute(slab, AXES, plane_to_column())  7.19 us
    pallas_call x1, Pallas kernels, shards(): pl.pallas_call(prepare_kernel, out_shape=(jax.ShapeDtypeStruct((kinship.s...  3.05 us
  transfers between devices with their start and end apart: 1, of which 0 were waited for; matrix products, arithmetic and copies ran while one was open for 0% of the time, Pallas kernels for 6%

profile of v12, /device:TPU:1, one launch (start us, length us, event | category | flops | bytes accessed | tf_op | source)
XLA Modules:
  0.0 53.8 jit_solution(2494336188394321475)
XLA Ops:
  0.6 0.0 copy-start
  0.6 0.7 %copy-done = f32[16,64]{1,0:T(8,128)S(1)} copy-done((f32[16,64]{1,0:T(8,128)S(1)}, f32[16,64]{1,0:T(8,128)}, u32[]{:S(2)}) %copy-start) | copy-done | bytes 4120
  1.3 0.1 pack.1
  1.4 16.0 %all_to_all.15.slab_ref = f32[32,8,128]{2,1,0:T(8,128)S(1)} all-to-all(f32[32,8,128]{2,1,0:T(8,128)S(1)} %pack.1), channel_id=1, replica_groups=mesh['z'=8,'x'=4,'y'=4,'c'=2] {'x','y','c'}, dimensions={0} | all-to-all | bytes 262144 | tf_op jit(solution)/shard_map/all_to_all | solution.py:146
  17.5 7.2 %collective-permute-start = (f32[32,8,128]{2,1,0:T(8,128)S(1)}, f32[32,8,128]{2,1,0:T(8,128)S(1)}, u32[]{:S(2)}, u32[]{:S(2)}) collective-permute-start(f32[32,8,128]{2,1,0:T(8,128)S(1)} %all_to_all.15.slab_ref), channel_id=1, source_target_pairs={{6,0},{2,32},{5,64},{0,96},{1,128},{3,160},{7,192},{4,224},{14,8},... | collective-permute-start | bytes 393224 | tf_op jit(solution)/shard_map/ppermute | solution.py:147
  24.6 3.0 %prepare.1 = (bf16[2048,640]{1,0:T(8,128)(2,1)S(1)}, bf16[2048,512]{1,0:T(8,128)(2,1)S(1)}) custom-call(f32[32,8,128]{2,1,0:T(8,128)S(1)} %all_to_all.15.slab_ref, f32[512,2048]{1,0:T(8,128)} %kinship_ref.1), custom_call_target="tpu_custom_call" | custom-call | tf_op jit(solution)/shard_map/prepare/pallas_call | solution.py:148
  27.7 0.0 collective-permute-done.block_ref
  27.7 1.0 %product.1 = f32[8,5,2,128]{3,2,1,0:T(2,128)S(1)} custom-call(f32[32,8,128]{2,1,0:T(8,128)S(1)} %collective-permute-done.block_ref, bf16[2048,640]{1,0:T(8,128)(2,1)S(1)} %get-tuple-element.6.high_ref, bf16[2048,512]{1,0:T(8,128)(2,1)S(1)} %get-tuple-element.7.low_ref), custom_call_target="tpu_custom_call" | custom-call | tf_op jit(solution)/shard_map/product/pallas_call | solution.py:160
  28.7 8.7 %all_to_all.16.parts_ref = f32[8,5,2,128]{3,2,1,0:T(2,128)S(1)} all-to-all(f32[8,5,2,128]{3,2,1,0:T(2,128)S(1)} %product.1), channel_id=1, replica_groups=mesh['z'=8,'x'=4,'y'=4,'c'=2] {'y','c'}, dimensions={0} | all-to-all | bytes 81920 | tf_op jit(solution)/shard_map/all_to_all | solution.py:168
  37.4 15.6 %all_to_all.17.refs_1_ = f32[32,2,128]{2,1,0:T(2,128)S(1)} all-to-all(f32[32,2,128]{2,1,0:T(2,128)S(1)} %get-tuple-element.9), channel_id=1, replica_groups=mesh['z'=8,'x'=4,'y'=4,'c'=2] {'z','x'}, dimensions={0} | all-to-all | bytes 65536 | tf_op jit(solution)/shard_map/all_to_all | solution.py:177
  53.0 0.8 %result.1 = (f32[16,64]{1,0:T(8,128)}, f32[16,16]{1,0:T(8,128)}) custom-call(f32[8,128]{1,0:T(8,128)S(1)} %get-tuple-element.8.refs_0_, f32[32,2,128]{2,1,0:T(2,128)S(1)} %all_to_all.17.refs_1_), custom_call_target="tpu_custom_call" | custom-call | tf_op jit(solution)/shard_map/result/pallas_call | solution.py:179
  (1 shorter events, 0.0 us)
Async XLA Ops:
  0.6 0.7 %copy-start = (f32[16,64]{1,0:T(8,128)S(1)}, f32[16,64]{1,0:T(8,128)}, u32[]{:S(2)}) copy-start(f32[16,64]{1,0:T(8,128)} %panel_ref.1) | copy-start | bytes 12292
  17.5 10.2 %collective-permute-start = (f32[32,8,128]{2,1,0:T(8,128)S(1)}, f32[32,8,128]{2,1,0:T(8,128)S(1)}, u32[]{:S(2)}, u32[]{:S(2)}) collective-permute-start(f32[32,8,128]{2,1,0:T(8,128)S(1)} %all_to_all.15.slab_ref), channel_id=1, source_target_pairs={{6,0},{2,32},{5,64},{0,96},{1,128},{3,160},{7,192},{4,224},{14,8},... | collective-permute-start | bytes 393224 | tf_op jit(solution)/shard_map/ppermute | solution.py:147

commit v13 on v12

--- a/solution.py
+++ b/solution.py
@@ -26,14 +26,14 @@
 
 
 SENDER = (
-    (6, 2, 5, 0, 1, 3, 7, 4),
-    (5, 4, 3, 2, 7, 0, 1, 6),
-    (0, 6, 1, 7, 4, 2, 3, 5),
-    (2, 1, 6, 5, 7, 4, 0, 3),
-    (4, 7, 2, 1, 3, 0, 6, 5),
-    (7, 5, 4, 2, 0, 6, 3, 1),
-    (3, 0, 7, 1, 4, 2, 5, 6),
-    (0, 2, 5, 6, 7, 4, 3, 1),
+    (6, 3, 5, 1, 0, 2, 4, 7),
+    (4, 5, 2, 3, 7, 1, 6, 0),
+    (1, 7, 0, 6, 2, 4, 3, 5),
+    (2, 0, 5, 7, 4, 6, 1, 3),
+    (4, 7, 0, 3, 1, 2, 6, 5),
+    (2, 5, 3, 4, 1, 6, 0, 7),
+    (0, 6, 7, 1, 5, 3, 4, 2),
+    (3, 0, 4, 6, 7, 5, 1, 2),
 )
 
 

time: 54 us -> 54.9 us (1.017)
  blocking collectives: 40.3 us -> 43.8 us
  starting transfers between devices: 7.19 us -> 4.62 us
    all_to_all x1, blocking collectives: 8.71 us -> 11.6 us  [shards(): parts = lax.all_to_all(parts, COLS, 0, 0, tiled=True)]
    ppermute x1, starting transfers between devices: 7.19 us -> 4.62 us  [shards(): block = lax.ppermute(slab, AXES, plane_to_column())]
where the time goes in v13:
time: 54.9 us; the launch traced here: 54.6 us
  blocking collectives  43.8 us (80%)
  Pallas kernels  4.9 us (9%)
  starting transfers between devices  4.62 us (8%)
  local copies, waits for them, and re-layouts  0.69 us (1%)
  between operations  0.66 us (1%)
    all_to_all x1, blocking collectives, shards(): scores = lax.all_to_all(scores, ROWS, 0, 0, tiled=True)  16.1 us
    all_to_all x1, blocking collectives, shards(): slab = lax.all_to_all(pieces, PLANE, 0, 0, tiled=True)  16 us
    all_to_all x1, blocking collectives, shards(): parts = lax.all_to_all(parts, COLS, 0, 0, tiled=True)  11.6 us
    ppermute x1, starting transfers between devices, shards(): block = lax.ppermute(slab, AXES, plane_to_column())  4.62 us
    pallas_call x1, Pallas kernels, shards(): pl.pallas_call(prepare_kernel, out_shape=(jax.ShapeDtypeStruct((kinship.s...  3.05 us
  transfers between devices with their start and end apart: 1, of which 0 were waited for; matrix products, arithmetic and copies ran while one was open for 0% of the time, Pallas kernels for 6%

profile of v13, /device:TPU:1, one launch (start us, length us, event | category | flops | bytes accessed | tf_op | source)
XLA Modules:
  0.0 54.6 jit_solution(12563678641314463581)
XLA Ops:
  0.6 0.0 copy-start
  0.6 0.7 %copy-done = f32[16,64]{1,0:T(8,128)S(1)} copy-done((f32[16,64]{1,0:T(8,128)S(1)}, f32[16,64]{1,0:T(8,128)}, u32[]{:S(2)}) %copy-start) | copy-done | bytes 4120
  1.3 0.1 pack.1
  1.4 16.0 %all_to_all.15.slab_ref = f32[32,8,128]{2,1,0:T(8,128)S(1)} all-to-all(f32[32,8,128]{2,1,0:T(8,128)S(1)} %pack.1), channel_id=1, replica_groups=mesh['z'=8,'x'=4,'y'=4,'c'=2] {'x','y','c'}, dimensions={0} | all-to-all | bytes 262144 | tf_op jit(solution)/shard_map/all_to_all | solution.py:146
  17.5 4.6 %collective-permute-start = (f32[32,8,128]{2,1,0:T(8,128)S(1)}, f32[32,8,128]{2,1,0:T(8,128)S(1)}, u32[]{:S(2)}, u32[]{:S(2)}) collective-permute-start(f32[32,8,128]{2,1,0:T(8,128)S(1)} %all_to_all.15.slab_ref), channel_id=1, source_target_pairs={{6,0},{3,32},{5,64},{1,96},{0,128},{2,160},{4,192},{7,224},{14,8},... | collective-permute-start | bytes 393224 | tf_op jit(solution)/shard_map/ppermute | solution.py:147
  22.1 3.0 %prepare.1 = (bf16[2048,640]{1,0:T(8,128)(2,1)S(1)}, bf16[2048,512]{1,0:T(8,128)(2,1)S(1)}) custom-call(f32[32,8,128]{2,1,0:T(8,128)S(1)} %all_to_all.15.slab_ref, f32[512,2048]{1,0:T(8,128)} %kinship_ref.1), custom_call_target="tpu_custom_call" | custom-call | tf_op jit(solution)/shard_map/prepare/pallas_call | solution.py:148
  25.1 0.0 collective-permute-done.block_ref
  25.1 1.0 %product.1 = f32[8,5,2,128]{3,2,1,0:T(2,128)S(1)} custom-call(f32[32,8,128]{2,1,0:T(8,128)S(1)} %collective-permute-done.block_ref, bf16[2048,640]{1,0:T(8,128)(2,1)S(1)} %get-tuple-element.6.high_ref, bf16[2048,512]{1,0:T(8,128)(2,1)S(1)} %get-tuple-element.7.low_ref), custom_call_target="tpu_custom_call" | custom-call | tf_op jit(solution)/shard_map/product/pallas_call | solution.py:160
  26.1 11.6 %all_to_all.16.parts_ref = f32[8,5,2,128]{3,2,1,0:T(2,128)S(1)} all-to-all(f32[8,5,2,128]{3,2,1,0:T(2,128)S(1)} %product.1), channel_id=1, replica_groups=mesh['z'=8,'x'=4,'y'=4,'c'=2] {'y','c'}, dimensions={0} | all-to-all | bytes 81920 | tf_op jit(solution)/shard_map/all_to_all | solution.py:168
  37.8 16.1 %all_to_all.17.refs_1_ = f32[32,2,128]{2,1,0:T(2,128)S(1)} all-to-all(f32[32,2,128]{2,1,0:T(2,128)S(1)} %get-tuple-element.9), channel_id=1, replica_groups=mesh['z'=8,'x'=4,'y'=4,'c'=2] {'z','x'}, dimensions={0} | all-to-all | bytes 65536 | tf_op jit(solution)/shard_map/all_to_all | solution.py:177
  53.9 0.8 %result.1 = (f32[16,64]{1,0:T(8,128)}, f32[16,16]{1,0:T(8,128)}) custom-call(f32[8,128]{1,0:T(8,128)S(1)} %get-tuple-element.8.refs_0_, f32[32,2,128]{2,1,0:T(2,128)S(1)} %all_to_all.17.refs_1_), custom_call_target="tpu_custom_call" | custom-call | tf_op jit(solution)/shard_map/result/pallas_call | solution.py:179
  (1 shorter events, 0.0 us)
Async XLA Ops:
  0.6 0.7 %copy-start = (f32[16,64]{1,0:T(8,128)S(1)}, f32[16,64]{1,0:T(8,128)}, u32[]{:S(2)}) copy-start(f32[16,64]{1,0:T(8,128)} %panel_ref.1) | copy-start | bytes 12292
  17.5 7.7 %collective-permute-start = (f32[32,8,128]{2,1,0:T(8,128)S(1)}, f32[32,8,128]{2,1,0:T(8,128)S(1)}, u32[]{:S(2)}, u32[]{:S(2)}) collective-permute-start(f32[32,8,128]{2,1,0:T(8,128)S(1)} %all_to_all.15.slab_ref), channel_id=1, source_target_pairs={{6,0},{3,32},{5,64},{1,96},{0,128},{2,160},{4,192},{7,224},{14,8},... | collective-permute-start | bytes 393224 | tf_op jit(solution)/shard_map/ppermute | solution.py:147

commit v14 on v13

--- a/solution.py
+++ b/solution.py
@@ -26,14 +26,14 @@
 
 
 SENDER = (
-    (6, 3, 5, 1, 0, 2, 4, 7),
-    (4, 5, 2, 3, 7, 1, 6, 0),
-    (1, 7, 0, 6, 2, 4, 3, 5),
-    (2, 0, 5, 7, 4, 6, 1, 3),
-    (4, 7, 0, 3, 1, 2, 6, 5),
-    (2, 5, 3, 4, 1, 6, 0, 7),
-    (0, 6, 7, 1, 5, 3, 4, 2),
-    (3, 0, 4, 6, 7, 5, 1, 2),
+    (4, 6, 3, 0, 1, 2, 7, 5),
+    (7, 4, 5, 2, 6, 1, 0, 3),
+    (1, 0, 6, 7, 4, 3, 2, 5),
+    (3, 0, 1, 7, 6, 4, 5, 2),
+    (5, 4, 2, 3, 0, 1, 6, 7),
+    (3, 4, 5, 2, 7, 0, 1, 6),
+    (1, 5, 7, 6, 4, 0, 3, 2),
+    (3, 1, 4, 7, 6, 0, 5, 2),
 )
 
 

time: 54.9 us -> 55.2 us (level)
  starting transfers between devices: 4.62 us -> 7.19 us
  blocking collectives: 43.8 us -> 41.5 us
    all_to_all x1, blocking collectives: 11.6 us -> 8.65 us  [shards(): parts = lax.all_to_all(parts, COLS, 0, 0, tiled=True)]
    ppermute x1, starting transfers between devices: 4.62 us -> 7.19 us  [shards(): block = lax.ppermute(slab, AXES, plane_to_column())]
    all_to_all x1, blocking collectives: 16.1 us -> 16.8 us  [shards(): scores = lax.all_to_all(scores, ROWS, 0, 0, tiled=True)]
where the time goes in v14:
time: 55.2 us; the launch traced here: 54.9 us
  blocking collectives  41.5 us (75%)
  starting transfers between devices  7.19 us (13%)
  Pallas kernels  4.9 us (9%)
  local copies, waits for them, and re-layouts  0.69 us (1%)
  between operations  0.66 us (1%)
    all_to_all x1, blocking collectives, shards(): scores = lax.all_to_all(scores, ROWS, 0, 0, tiled=True)  16.8 us
    all_to_all x1, blocking collectives, shards(): slab = lax.all_to_all(pieces, PLANE, 0, 0, tiled=True)  16 us
    all_to_all x1, blocking collectives, shards(): parts = lax.all_to_all(parts, COLS, 0, 0, tiled=True)  8.65 us
    ppermute x1, starting transfers between devices, shards(): block = lax.ppermute(slab, AXES, plane_to_column())  7.19 us
    pallas_call x1, Pallas kernels, shards(): pl.pallas_call(prepare_kernel, out_shape=(jax.ShapeDtypeStruct((kinship.s...  3.05 us
  transfers between devices with their start and end apart: 1, of which 0 were waited for; matrix products, arithmetic and copies ran while one was open for 0% of the time, Pallas kernels for 6%

profile of v14, /device:TPU:1, one launch (start us, length us, event | category | flops | bytes accessed | tf_op | source)
XLA Modules:
  0.0 54.9 jit_solution(14503814260000742905)
XLA Ops:
  0.6 0.0 copy-start
  0.6 0.7 %copy-done = f32[16,64]{1,0:T(8,128)S(1)} copy-done((f32[16,64]{1,0:T(8,128)S(1)}, f32[16,64]{1,0:T(8,128)}, u32[]{:S(2)}) %copy-start) | copy-done | bytes 4120
  1.3 0.1 pack.1
  1.4 16.0 %all_to_all.15.slab_ref = f32[32,8,128]{2,1,0:T(8,128)S(1)} all-to-all(f32[32,8,128]{2,1,0:T(8,128)S(1)} %pack.1), channel_id=1, replica_groups=mesh['z'=8,'x'=4,'y'=4,'c'=2] {'x','y','c'}, dimensions={0} | all-to-all | bytes 262144 | tf_op jit(solution)/shard_map/all_to_all | solution.py:146
  17.5 7.2 %collective-permute-start = (f32[32,8,128]{2,1,0:T(8,128)S(1)}, f32[32,8,128]{2,1,0:T(8,128)S(1)}, u32[]{:S(2)}, u32[]{:S(2)}) collective-permute-start(f32[32,8,128]{2,1,0:T(8,128)S(1)} %all_to_all.15.slab_ref), channel_id=1, source_target_pairs={{4,0},{6,32},{3,64},{0,96},{1,128},{2,160},{7,192},{5,224},{12,8},... | collective-permute-start | bytes 393224 | tf_op jit(solution)/shard_map/ppermute | solution.py:147
  24.6 3.0 %prepare.1 = (bf16[2048,640]{1,0:T(8,128)(2,1)S(1)}, bf16[2048,512]{1,0:T(8,128)(2,1)S(1)}) custom-call(f32[32,8,128]{2,1,0:T(8,128)S(1)} %all_to_all.15.slab_ref, f32[512,2048]{1,0:T(8,128)} %kinship_ref.1), custom_call_target="tpu_custom_call" | custom-call | tf_op jit(solution)/shard_map/prepare/pallas_call | solution.py:148
  27.7 0.0 collective-permute-done.block_ref
  27.7 1.0 %product.1 = f32[8,5,2,128]{3,2,1,0:T(2,128)S(1)} custom-call(f32[32,8,128]{2,1,0:T(8,128)S(1)} %collective-permute-done.block_ref, bf16[2048,640]{1,0:T(8,128)(2,1)S(1)} %get-tuple-element.6.high_ref, bf16[2048,512]{1,0:T(8,128)(2,1)S(1)} %get-tuple-element.7.low_ref), custom_call_target="tpu_custom_call" | custom-call | tf_op jit(solution)/shard_map/product/pallas_call | solution.py:160
  28.7 8.7 %all_to_all.16.parts_ref = f32[8,5,2,128]{3,2,1,0:T(2,128)S(1)} all-to-all(f32[8,5,2,128]{3,2,1,0:T(2,128)S(1)} %product.1), channel_id=1, replica_groups=mesh['z'=8,'x'=4,'y'=4,'c'=2] {'y','c'}, dimensions={0} | all-to-all | bytes 81920 | tf_op jit(solution)/shard_map/all_to_all | solution.py:168
  37.4 16.8 %all_to_all.17.refs_1_ = f32[32,2,128]{2,1,0:T(2,128)S(1)} all-to-all(f32[32,2,128]{2,1,0:T(2,128)S(1)} %get-tuple-element.9), channel_id=1, replica_groups=mesh['z'=8,'x'=4,'y'=4,'c'=2] {'z','x'}, dimensions={0} | all-to-all | bytes 65536 | tf_op jit(solution)/shard_map/all_to_all | solution.py:177
  54.1 0.8 %result.1 = (f32[16,64]{1,0:T(8,128)}, f32[16,16]{1,0:T(8,128)}) custom-call(f32[8,128]{1,0:T(8,128)S(1)} %get-tuple-element.8.refs_0_, f32[32,2,128]{2,1,0:T(2,128)S(1)} %all_to_all.17.refs_1_), custom_call_target="tpu_custom_call" | custom-call | tf_op jit(solution)/shard_map/result/pallas_call | solution.py:179
  (1 shorter events, 0.0 us)
Async XLA Ops:
  0.6 0.7 %copy-start = (f32[16,64]{1,0:T(8,128)S(1)}, f32[16,64]{1,0:T(8,128)}, u32[]{:S(2)}) copy-start(f32[16,64]{1,0:T(8,128)} %panel_ref.1) | copy-start | bytes 12292
  17.5 10.2 %collective-permute-start = (f32[32,8,128]{2,1,0:T(8,128)S(1)}, f32[32,8,128]{2,1,0:T(8,128)S(1)}, u32[]{:S(2)}, u32[]{:S(2)}) collective-permute-start(f32[32,8,128]{2,1,0:T(8,128)S(1)} %all_to_all.15.slab_ref), channel_id=1, source_target_pairs={{4,0},{6,32},{3,64},{0,96},{1,128},{2,160},{7,192},{5,224},{12,8},... | collective-permute-start | bytes 393224 | tf_op jit(solution)/shard_map/ppermute | solution.py:147
